TPU v7x, 512 devices: a whole 4x8x8 slice. The times are simulated.
512 devices in a mesh: req: 128 (over y, z, core), tp: 4 (over x).
Axes of the slice: x: 4, y: 8, z: 8, core: 2. Of those that a mesh axis runs over, the one named last changes fastest.
Arguments:
- tokens: bfloat16 [16384, 1024], P('req'), may hold values from -6 to 6
- attn_heads: bfloat16 [16384, 1024], P('req', 'tp'), may hold values from -6 to 6
- out_proj: bfloat16 [1024, 1024], P('tp'), may hold values from -0.1875 to 0.1875
- norm_gain: float32 [1024], replicated, may hold values from 0.3 to 1.7
- w_gate: bfloat16 [32, 1024, 512], P(None, 'req', 'tp'), may hold values from -0.1875 to 0.1875
- w_up: bfloat16 [32, 1024, 512], P(None, 'req', 'tp'), may hold values from -0.1875 to 0.1875
- w_down: bfloat16 [32, 1024, 512], P(None, 'req', 'tp'), may hold values from -0.25 to 0.25
- routes: int32 [16384, 8], P('req'), may hold values from 0 to 31, all different within a row; in each aligned block of 32 rows (0 to 31, 32 to 63, ...) at most 12 rows name the same one
- gate_weights: float32 [16384, 8], P('req'), may hold values from 0.05 to 0.45
- cache_pages: bfloat16 [1024, 128, 8, 128], P('req', None, 'tp'), may hold values from -6 to 6
- page_dest: int32 [1024], P('req'), may hold values from 0 to 1023, as said below
Outputs:
- layer_output: bfloat16 [16384, 1024], P('req', 'tp')
- decode_cache: bfloat16 [1024, 128, 8, 128], P('req', None, 'tp')
Inputs may be any that keep to these rules, and one draw needn't show every extreme that they name: `routes`: within each aligned block of 32 rows no expert is named by more than 12 rows, and some block reaches 12. The page p of index r of req (p among its 8 pages) is sent to the index r + k modulo 128 for some k from 0 to 7, into its decode slot k: page_dest[p] = ((r + k) % 128) * 8 + k. The 8 pages of one index use each k once, so every decode slot gets one page.
All inputs are finite; a program needn't handle non-finite values.
Results may differ from a plain program's by a relative error of at most 0.012.
Values may be sent and summed in bfloat16 or wider, within the bound.
A program may use at most 64 MiB of HBM per device.

v0:
```python
import jax
import jax.numpy as jnp
import numpy as np
from jax import lax
from jax.sharding import PartitionSpec as P


def passed_along(value, axis, steps):
    count = lax.axis_size(axis)
    pairs = [(source, (source + steps) % count) for source in range(count)]
    return lax.ppermute(value, axis, pairs)


def on_device(
    tokens,
    attn_heads,
    out_proj,
    norm_gain,
    w_gate,
    w_up,
    w_down,
    routes,
    gate_weights,
    cache_pages,
    page_dest,
):
    req_count = lax.axis_size("req")
    tp_count = lax.axis_size("tp")
    tp_place = lax.axis_index("tp")
    tok_count, top_count = routes.shape
    experts = w_gate.shape[0]
    model_width = tokens.shape[1]
    quarter_width = model_width // tp_count
    partial_value = jnp.dot(attn_heads, out_proj, preferred_element_type=jnp.float32)
    attention = lax.psum(partial_value.astype(jnp.bfloat16), "tp").astype(jnp.float32)
    residual = tokens.astype(jnp.float32) + attention
    inverse = lax.rsqrt(jnp.mean(residual * residual, axis=1, keepdims=True) + 1e-05)
    normed = (residual * inverse * norm_gain).astype(jnp.bfloat16)
    resid_part = lax.dynamic_slice_in_dim(residual, tp_place * quarter_width, quarter_width, 1)
    local_experts = max(1, experts // req_count)
    expert_groups = experts // local_experts
    replicas = req_count // expert_groups
    block_rows = tok_count // replicas
    capacity = 3 * block_rows * top_count // (2 * experts)
    slot_total = req_count * local_experts * capacity
    expert_ids = jnp.arange(experts, dtype=jnp.int32)
    token_hits = jnp.sum((routes[:, :, None] == expert_ids).astype(jnp.int32), axis=1)
    blocked = token_hits.reshape(replicas, block_rows, experts)
    earlier = (jnp.cumsum(blocked, axis=1) - blocked).reshape(tok_count, experts)
    slot_rank = jnp.take_along_axis(earlier, routes, axis=1)
    row_ids = jnp.arange(tok_count, dtype=jnp.int32)[:, None]
    target = row_ids // block_rows * expert_groups + routes // local_experts
    slot_ids = (target * local_experts + routes % local_experts) * capacity + slot_rank
    flat_slots = slot_ids.reshape(-1)
    flat_rows = jnp.broadcast_to(row_ids, slot_ids.shape).reshape(-1)
    slot_token = jnp.zeros((slot_total,), jnp.int32).at[flat_slots].set(flat_rows)
    slot_live = jnp.zeros((slot_total,), jnp.bfloat16).at[flat_slots].set(1.0)
    owner_table = (
        np.arange(req_count)[:, None] % expert_groups * local_experts
        + np.arange(local_experts)[None, :]
    )
    outgoing = (w_gate[owner_table], w_up[owner_table], w_down[owner_table])
    gate_full, up_full, down_full = (
        lax.all_to_all(outgoing[0], "req", split_axis=0, concat_axis=2, tiled=True),
        lax.all_to_all(outgoing[1], "req", split_axis=0, concat_axis=2, tiled=True),
        lax.all_to_all(outgoing[2], "req", split_axis=0, concat_axis=2, tiled=True),
    )
    gate_full = gate_full[0]
    up_full = up_full[0]
    down_full = down_full[0]
    outbox = (normed[slot_token] * slot_live[:, None]).reshape(
        req_count, local_experts, capacity, model_width
    )
    arrived = lax.all_to_all(outbox, "req", split_axis=0, concat_axis=0, tiled=True)
    pre_gate = jnp.einsum("recd,edh->rech", arrived, gate_full, preferred_element_type=jnp.float32)
    pre_up = jnp.einsum("recd,edh->rech", arrived, up_full, preferred_element_type=jnp.float32)
    active = (jax.nn.silu(pre_gate) * pre_up).astype(jnp.bfloat16)
    pieces = jnp.einsum(
        "rech,edh->recd", active, down_full, preferred_element_type=jnp.float32
    ).astype(jnp.bfloat16)
    returned = lax.all_to_all(pieces, "req", split_axis=0, concat_axis=0, tiled=True)
    gathered = returned.reshape(slot_total, model_width)[slot_ids]
    combined = jnp.sum(gate_weights[:, :, None] * gathered.astype(jnp.float32), axis=1)
    mixture = lax.psum_scatter(
        combined.astype(jnp.bfloat16), "tp", scatter_dimension=1, tiled=True
    ).astype(jnp.float32)
    layer_output = (resid_part + mixture).astype(jnp.bfloat16)
    spread = cache_pages.shape[0]
    page_offsets = page_dest % spread
    page_order = (
        jnp.zeros((spread,), jnp.int32).at[page_offsets].set(jnp.arange(spread, dtype=jnp.int32))
    )
    ranked = cache_pages[page_order]
    arrived_pages = [ranked[0]]
    for offset in range(1, spread):
        arrived_pages.append(passed_along(ranked[offset], "req", offset))
    decode_cache = jnp.stack(arrived_pages)
    return (layer_output, decode_cache)


def solution(mesh):
    in_specs = (
        P("req", None),
        P("req", "tp"),
        P("tp", None),
        P(),
        P(None, "req", "tp"),
        P(None, "req", "tp"),
        P(None, "req", "tp"),
        P("req", None),
        P("req", None),
        P("req", None, "tp", None),
        P("req"),
    )
    out_specs = (P("req", "tp"), P("req", None, "tp", None))
    return jax.shard_map(
        on_device, mesh=mesh, in_specs=in_specs, out_specs=out_specs, check_vma=False
    )
```

profile of v0, /device:TPU:1, one launch (start us, length us, event | category | flops | bytes accessed | tf_op | source)
XLA Modules:
  0.0 436.5 jit_solution(17030307056659740838)
XLA Ops:
  13.5 18.4 %all-to-all-start.1 = ((bf16[128,1,8,128]{3,2,1,0:T(8,128)(2,1)}), bf16[128,1,8,128]{3,2,1,0:T(8,128)(2,1)S(1)}, u32[]{:S(2)}, u32[]{:S(2)}) async-start(bf16[128,1,8,128]{3,2,1,0:T(8,128)(2,1)} %bitcast.3), calls=%async_computation.1 | async-start | bytes 524288 | tf_op jit(solution)/shard_map/all_to_all | solution.py:64
  33.7 7.1 %gather_fusion.6 = s32[1024]{0:T(1024)S(1)} fusion(s32[128,32]{1,0:T(8,128)S(1)} %bitcast_subtract_fusion, s32[1024]{0:T(1024)S(1)} %reshape.217), kind=kCustom, calls=%fused_computation.6 | custom fusion | bytes 16384 | tf_op jit(solution)/shard_map/jit(take_along_axis)/gather | solution.py:50
  41.3 4.3 scatter_custom_fusion
  45.7 7.6 %scatter_custom_fusion.1 = bf16[1536]{0:T(1024)(128)(2,1)S(1)} fusion(s32[1024]{0:T(1024)S(1)} %bitcast.105, bf16[1024]{0:T(1024)(128)(2,1)S(1)} %broadcast.148, bf16[]{:T(256)} %constant.106.clone.1), kind=kCustom, calls=%fused_computation.73 | custom fusion | bytes 3074 | tf_op jit(solution)/shard_map/scatter | solution.py:57
  54.8 11.9 %all-reduce.2.cloned.1.call-done = bf16[128,1024]{1,0:T(8,128)(2,1)} async-done(((bf16[128,1024]{1,0:T(8,128)(2,1)}), bf16[128,1024]{1,0:T(8,128)(2,1)}) %all-reduce.2.cloned.1.call-update) | async-done | bytes 262160 | tf_op jit(solution)/shard_map/psum | solution.py:35
  67.8 16.4 %all-to-all-start.3 = ((bf16[128,1,8,128]{3,2,1,0:T(8,128)(2,1)}), bf16[128,1,8,128]{3,2,1,0:T(8,128)(2,1)S(1)}, u32[]{:S(2)}, u32[]{:S(2)}) async-start(bf16[128,1,8,128]{3,2,1,0:T(8,128)(2,1)} %bitcast.15), calls=%async_computation.3 | async-start | bytes 524288 | tf_op jit(solution)/shard_map/all_to_all | solution.py:65
  85.3 5.8 %gather_fusion.2 = bf16[1536,1024]{1,0:T(8,128)(2,1)} fusion(bf16[128,1024]{1,0:T(8,128)(2,1)S(1)} %multiply_convert_fusion, s32[2048]{0:T(1024)S(1)} %pad_clamp_fusion), kind=kCustom, calls=%fused_computation.2 | custom fusion | bytes 6297600 | tf_op jit(solution)/shard_map/gather | solution.py:71
  91.1 6.1 %gather.28 = bf16[128,1,12,1024]{3,2,0,1:T(8,128)(2,1)} reshape(bf16[1536,1024]{1,0:T(8,128)(2,1)} %gather_fusion.2) | data formatting | bytes 6291456 | tf_op jit(solution)/shard_map/gather | solution.py:71
  97.2 4.5 %multiply_bitcast_fusion = bf16[128,1,12,1024]{3,2,1,0:T(8,128)(2,1)} fusion(bf16[128,1,12,1024]{3,2,0,1:T(8,128)(2,1)} %gather.28, bf16[128,12]{1,0:T(8,128)(2,1)S(1)} %mul.78), kind=kLoop, calls=%fused_computation.12 | loop fusion | flops 1572864 | bytes 6294528 | tf_op jit(solution)/shard_map/mul | solution.py:71
  101.7 14.3 %all-to-all-start.2 = ((bf16[128,1,12,1024]{3,2,1,0:T(8,128)(2,1)}), bf16[128,1,12,1024]{3,2,1,0:T(8,128)(2,1)}, u32[]{:S(2)}, u32[]{:S(2)}) async-start(bf16[128,1,12,1024]{3,2,1,0:T(8,128)(2,1)} %multiply_bitcast_fusion), calls=%async_computation.2 | async-start | bytes 8388608 | tf_op jit(solution)/shard_map/all_to_all | solution.py:74
  117.4 94.2 %all-to-all-done.2 = bf16[128,1,12,1024]{3,2,1,0:T(8,128)(2,1)} async-done(((bf16[128,1,12,1024]{3,2,1,0:T(8,128)(2,1)}), bf16[128,1,12,1024]{3,2,1,0:T(8,128)(2,1)}, u32[]{:S(2)}, u32[]{:S(2)}) %all-to-all-start.2) | async-done | bytes 3145760 | tf_op jit(solution)/shard_map/all_to_all | solution.py:74
  211.5 17.3 %all-to-all-start = ((bf16[128,1,8,128]{3,2,1,0:T(8,128)(2,1)}), bf16[128,1,8,128]{3,2,1,0:T(8,128)(2,1)S(1)}, u32[]{:S(2)}, u32[]{:S(2)}) async-start(bf16[128,1,8,128]{3,2,1,0:T(8,128)(2,1)} %bitcast), calls=%async_computation | async-start | bytes 524288 | tf_op jit(solution)/shard_map/all_to_all | solution.py:66
  228.8 5.8 %fusion.7 = f32[128,1,12,128]{0,3,2,1:T(8,128)S(1)} fusion(bf16[128,1,12,1024]{3,2,1,0:T(8,128)(2,1)} %all-to-all-done.2, bf16[128,1,8,128]{3,2,1,0:T(8,128)(2,1)S(1)} %all-to-all-done.1), kind=kOutput, calls=%fused_computation.20 | convolution fusion | flops 402653184 | bytes 4194304 | tf_op jit(solution)/shard_map/recd,edh->rech/dot_general | solution.py:75
  234.6 8.4 %all-to-all-done = bf16[128,1,8,128]{3,2,1,0:T(8,128)(2,1)S(1)} async-done(((bf16[128,1,8,128]{3,2,1,0:T(8,128)(2,1)}), bf16[128,1,8,128]{3,2,1,0:T(8,128)(2,1)S(1)}, u32[]{:S(2)}, u32[]{:S(2)}) %all-to-all-start) | async-done | bytes 262176 | tf_op jit(solution)/shard_map/all_to_all | solution.py:66
  243.0 8.4 %convert_bitcast_fusion = bf16[128,1,12,1024]{0,3,2,1:T(8,128)(2,1)} fusion(bf16[128,1,12,1024]{3,2,1,0:T(8,128)(2,1)} %all-to-all-done.2, f32[128,1,12,128]{0,3,2,1:T(8,128)S(1)} %fusion.7, bf16[128,1,8,128]{3,2,1,0:T(8,128)(2,1)S(1)} %all-to-all-done.3, bf16[128,1,8,128]{3,2,1,0:T(8,128)(2,1)S(1)} %all-to-all-done), kind=kOutput, calls=%fused_computation.17 | convolution fusion | flops 808058880 | bytes 7602176 | tf_op jit(solution)/shard_map/rech,edh->recd/dot_general | solution.py:78
  251.4 6.5 %copy.82 = bf16[128,1,12,1024]{3,2,1,0:T(8,128)(2,1)} copy(bf16[128,1,12,1024]{0,3,2,1:T(8,128)(2,1)} %convert_bitcast_fusion) | data formatting | bytes 6291456 | tf_op jit(solution)/shard_map/convert_element_type | solution.py:80
  257.9 8.2 %all-to-all-start.4 = ((bf16[128,1,12,1024]{3,2,1,0:T(8,128)(2,1)}), bf16[128,1,12,1024]{3,2,1,0:T(8,128)(2,1)}, u32[]{:S(2)}, u32[]{:S(2)}) async-start(bf16[128,1,12,1024]{3,2,1,0:T(8,128)(2,1)} %copy.82), calls=%async_computation.4 | async-start | bytes 8388608 | tf_op jit(solution)/shard_map/all_to_all | solution.py:81
  278.4 4.3 collective-permute-start.3
  286.6 7.3 %collective-permute-done = bf16[128,2,128]{2,1,0:T(2,128)(2,1)S(1)} collective-permute-done((bf16[128,2,128]{2,1,0:T(2,128)(2,1)S(1)}, bf16[128,2,128]{2,1,0:T(2,128)(2,1)S(1)}, u32[]{:S(2)}, u32[]{:S(2)}) %collective-permute-start) | collective-permute-done | bytes 65568 | tf_op jit(solution)/shard_map/ppermute | solution.py:11
  293.9 47.3 %collective-permute-start.5 = (bf16[128,2,128]{2,1,0:T(2,128)(2,1)S(1)}, bf16[128,2,128]{2,1,0:T(2,128)(2,1)S(1)}, u32[]{:S(2)}, u32[]{:S(2)}) collective-permute-start(bf16[128,2,128]{2,1,0:T(2,128)(2,1)S(1)} %get-tuple-element.5), channel_id=1, source_target_pairs={{0,24},{4,28},{8,32},{12,36},{16,40},{20,44},{24,48},{28,52},{32,5... | collective-permute-start | bytes 196616 | tf_op jit(solution)/shard_map/ppermute | solution.py:11
  341.3 25.2 %collective-permute-done.1 = bf16[128,2,128]{2,1,0:T(2,128)(2,1)S(1)} collective-permute-done((bf16[128,2,128]{2,1,0:T(2,128)(2,1)S(1)}, bf16[128,2,128]{2,1,0:T(2,128)(2,1)S(1)}, u32[]{:S(2)}, u32[]{:S(2)}) %collective-permute-start.1) | collective-permute-done | bytes 65568 | tf_op jit(solution)/shard_map/ppermute | solution.py:11
  370.1 6.1 %reshape.168 = bf16[1536,1024]{1,0:T(8,128)(2,1)} reshape(bf16[128,1,12,1024]{3,2,1,0:T(8,128)(2,1)} %all-to-all-done.4) | data formatting | bytes 6291456 | tf_op jit(solution)/shard_map/reshape | solution.py:82
  376.2 7.3 %gather_fusion.4 = bf16[1024,1024]{1,0:T(8,128)(2,1)S(1)} fusion(bf16[1536,1024]{1,0:T(8,128)(2,1)} %reshape.168, s32[1024]{0:T(1024)S(1)} %broadcast_clamp_fusion), kind=kCustom, calls=%fused_computation.4 | custom fusion | bytes 4198400 | tf_op jit(solution)/shard_map/gather | solution.py:82
  388.4 39.7 %reduce-scatter.2.cloned.1.call-done = bf16[128,256]{1,0:T(8,128)(2,1)} async-done(((bf16[128,1024]{1,0:T(8,128)(2,1)}), bf16[128,256]{1,0:T(8,128)(2,1)}) %reduce-scatter.2.cloned.1.call-update) | async-done | bytes 65552 | tf_op jit(solution)/shard_map/reduce_scatter | solution.py:84
  (80 shorter events, 39.6 us)
Async XLA Ops:
  7.2 259.3 %copy-start = (bf16[8,128,2,128]{3,2,1,0:T(2,128)(2,1)S(1)}, bf16[8,128,2,128]{3,2,1,0:T(2,128)(2,1)}, u32[]{:S(2)}) copy-start(bf16[8,128,2,128]{3,2,1,0:T(2,128)(2,1)} %param.24) | copy-start | bytes 1572868
  7.2 59.5 %all-reduce.2.cloned.1.call-start = ((), (), s32[]{:S(2)}) async-start(), calls=%async_computation.6 | async-start | bytes 524288 | tf_op jit(solution)/shard_map/psum | solution.py:35
  13.5 54.3 %all-to-all-start.1 = ((bf16[128,1,8,128]{3,2,1,0:T(8,128)(2,1)}), bf16[128,1,8,128]{3,2,1,0:T(8,128)(2,1)S(1)}, u32[]{:S(2)}, u32[]{:S(2)}) async-start(bf16[128,1,8,128]{3,2,1,0:T(8,128)(2,1)} %bitcast.3), calls=%async_computation.1 | async-start | bytes 524288 | tf_op jit(solution)/shard_map/all_to_all | solution.py:64
  33.7 7.3 %copy-start.4 = (s32[128,8]{0,1:T(8,128)S(1)}, s32[128,8]{0,1:T(8,128)}, u32[]{:S(2)}) copy-start(s32[128,8]{0,1:T(8,128)} %param.22) | copy-start | bytes 12292
  33.7 19.7 %copy-start.1 = (bf16[32,8,128]{2,1,0:T(8,128)(2,1)S(1)}, bf16[32,8,128]{2,1,0:T(8,128)(2,1)}, u32[]{:S(2)}) copy-start(bf16[32,8,128]{2,1,0:T(8,128)(2,1)} %param.20) | copy-start | bytes 196612
  33.7 33.0 %copy-start.3 = (bf16[128,1024]{1,0:T(8,128)(2,1)S(1)}, bf16[128,1024]{1,0:T(8,128)(2,1)}, u32[]{:S(2)}) copy-start(bf16[128,1024]{1,0:T(8,128)(2,1)} %param.15) | copy-start | bytes 786436
  33.7 50.5 %copy-start.6 = (f32[1024]{0:T(1024)S(1)}, f32[1024]{0:T(1024)}, u32[]{:S(2)}) copy-start(f32[1024]{0:T(1024)} %param.18) | copy-start | bytes 12292
  67.8 33.9 %all-to-all-start.3 = ((bf16[128,1,8,128]{3,2,1,0:T(8,128)(2,1)}), bf16[128,1,8,128]{3,2,1,0:T(8,128)(2,1)S(1)}, u32[]{:S(2)}, u32[]{:S(2)}) async-start(bf16[128,1,8,128]{3,2,1,0:T(8,128)(2,1)} %bitcast.15), calls=%async_computation.3 | async-start | bytes 524288 | tf_op jit(solution)/shard_map/all_to_all | solution.py:65
  101.7 14.3 %copy-start.2 = (bf16[32,8,128]{2,1,0:T(8,128)(2,1)S(1)}, bf16[32,8,128]{2,1,0:T(8,128)(2,1)}, u32[]{:S(2)}) copy-start(bf16[32,8,128]{2,1,0:T(8,128)(2,1)} %param.21) | copy-start | bytes 196612
  101.7 109.9 %all-to-all-start.2 = ((bf16[128,1,12,1024]{3,2,1,0:T(8,128)(2,1)}), bf16[128,1,12,1024]{3,2,1,0:T(8,128)(2,1)}, u32[]{:S(2)}, u32[]{:S(2)}) async-start(bf16[128,1,12,1024]{3,2,1,0:T(8,128)(2,1)} %multiply_bitcast_fusion), calls=%async_computation.2 | async-start | bytes 8388608 | tf_op jit(solution)/shard_map/all_to_all | solution.py:74
  211.5 31.5 %all-to-all-start = ((bf16[128,1,8,128]{3,2,1,0:T(8,128)(2,1)}), bf16[128,1,8,128]{3,2,1,0:T(8,128)(2,1)S(1)}, u32[]{:S(2)}, u32[]{:S(2)}) async-start(bf16[128,1,8,128]{3,2,1,0:T(8,128)(2,1)} %bitcast), calls=%async_computation | async-start | bytes 524288 | tf_op jit(solution)/shard_map/all_to_all | solution.py:66
  257.9 28.5 %copy-start.7 = (f32[128,8]{0,1:T(8,128)S(1)}, f32[128,8]{0,1:T(8,128)}, u32[]{:S(2)}) copy-start(f32[128,8]{0,1:T(8,128)} %param.23) | copy-start | bytes 12292
  257.9 111.4 %all-to-all-start.4 = ((bf16[128,1,12,1024]{3,2,1,0:T(8,128)(2,1)}), bf16[128,1,12,1024]{3,2,1,0:T(8,128)(2,1)}, u32[]{:S(2)}, u32[]{:S(2)}) async-start(bf16[128,1,12,1024]{3,2,1,0:T(8,128)(2,1)} %copy.82), calls=%async_computation.4 | async-start | bytes 8388608 | tf_op jit(solution)/shard_map/all_to_all | solution.py:81
  266.2 162.0 %reduce-scatter.2.cloned.1.call-start = ((), (), s32[]{:S(2)}) async-start(), calls=%async_computation.7 | async-start | bytes 327680 | tf_op jit(solution)/shard_map/reduce_scatter | solution.py:84
  268.4 25.5 %collective-permute-start = (bf16[128,2,128]{2,1,0:T(2,128)(2,1)S(1)}, bf16[128,2,128]{2,1,0:T(2,128)(2,1)S(1)}, u32[]{:S(2)}, u32[]{:S(2)}) collective-permute-start(bf16[128,2,128]{2,1,0:T(2,128)(2,1)S(1)} %get-tuple-element.10), channel_id=1, source_target_pairs={{0,4},{4,8},{8,12},{12,16},{16,20},{20,24},{24,28},{28,32},{32,36}... | collective-permute-start | bytes 196616 | tf_op jit(solution)/shard_map/ppermute | solution.py:11
  272.0 94.5 %collective-permute-start.1 = (bf16[128,2,128]{2,1,0:T(2,128)(2,1)S(1)}, bf16[128,2,128]{2,1,0:T(2,128)(2,1)S(1)}, u32[]{:S(2)}, u32[]{:S(2)}) collective-permute-start(bf16[128,2,128]{2,1,0:T(2,128)(2,1)S(1)} %get-tuple-element.9), channel_id=1, source_target_pairs={{0,8},{4,12},{8,16},{12,20},{16,24},{20,28},{24,32},{28,36},{32,40... | collective-permute-start | bytes 196616 | tf_op jit(solution)/shard_map/ppermute | solution.py:11
  275.1 93.4 %collective-permute-start.2 = (bf16[128,2,128]{2,1,0:T(2,128)(2,1)S(1)}, bf16[128,2,128]{2,1,0:T(2,128)(2,1)S(1)}, u32[]{:S(2)}, u32[]{:S(2)}) collective-permute-start(bf16[128,2,128]{2,1,0:T(2,128)(2,1)S(1)} %get-tuple-element.8), channel_id=1, source_target_pairs={{0,12},{4,16},{8,20},{12,24},{16,28},{20,32},{24,36},{28,40},{32,4... | collective-permute-start | bytes 196616 | tf_op jit(solution)/shard_map/ppermute | solution.py:11
  278.4 90.9 %collective-permute-start.3 = (bf16[128,2,128]{2,1,0:T(2,128)(2,1)S(1)}, bf16[128,2,128]{2,1,0:T(2,128)(2,1)S(1)}, u32[]{:S(2)}, u32[]{:S(2)}) collective-permute-start(bf16[128,2,128]{2,1,0:T(2,128)(2,1)S(1)} %get-tuple-element.7), channel_id=1, source_target_pairs={{0,16},{4,20},{8,24},{12,28},{16,32},{20,36},{24,40},{28,44},{32,4... | collective-permute-start | bytes 196616 | tf_op jit(solution)/shard_map/ppermute | solution.py:11
  282.7 102.8 %collective-permute-start.4 = (bf16[128,2,128]{2,1,0:T(2,128)(2,1)S(1)}, bf16[128,2,128]{2,1,0:T(2,128)(2,1)S(1)}, u32[]{:S(2)}, u32[]{:S(2)}) collective-permute-start(bf16[128,2,128]{2,1,0:T(2,128)(2,1)S(1)} %get-tuple-element.6), channel_id=1, source_target_pairs={{0,20},{4,24},{8,28},{12,32},{16,36},{20,40},{24,44},{28,48},{32,5... | collective-permute-start | bytes 196616 | tf_op jit(solution)/shard_map/ppermute | solution.py:11
  293.9 92.3 %collective-permute-start.5 = (bf16[128,2,128]{2,1,0:T(2,128)(2,1)S(1)}, bf16[128,2,128]{2,1,0:T(2,128)(2,1)S(1)}, u32[]{:S(2)}, u32[]{:S(2)}) collective-permute-start(bf16[128,2,128]{2,1,0:T(2,128)(2,1)S(1)} %get-tuple-element.5), channel_id=1, source_target_pairs={{0,24},{4,28},{8,32},{12,36},{16,40},{20,44},{24,48},{28,52},{32,5... | collective-permute-start | bytes 196616 | tf_op jit(solution)/shard_map/ppermute | solution.py:11
  366.5 20.4 %collective-permute-start.6 = (bf16[128,2,128]{2,1,0:T(2,128)(2,1)S(1)}, bf16[128,2,128]{2,1,0:T(2,128)(2,1)}, u32[]{:S(2)}, u32[]{:S(2)}) collective-permute-start(bf16[128,2,128]{2,1,0:T(2,128)(2,1)S(1)} %get-tuple-element.4), channel_id=1, source_target_pairs={{0,28},{4,32},{8,36},{12,40},{16,44},{20,48},{24,52},{28,56},{32,6... | collective-permute-start | bytes 196616 | tf_op jit(solution)/shard_map/ppermute | solution.py:11
  369.3 0.8 copy-start.5
Sparse Core Ops, SparseCore 0:
  10.9 55.7 all-reduce.1
  385.7 42.4 reduce-scatter.1
where the time goes:
time: 439 us; the launch traced here: 436 us
  waiting for transfers between devices  187 us (43%)
  starting transfers between devices  142 us (32%)
  local copies, waits for them, and re-layouts  63.4 us (14%)
  matrix products  16.2 us (4%)
  between operations  14.4 us (3%)
  other arithmetic  13 us (3%)
    all_to_all x1, waiting for transfers between devices, on_device(): lax.all_to_all(outbox, 'req', split_axis=0, concat_axis=0, tiled=True)  94.2 us
    ppermute x7, starting transfers between devices, passed_along(): return lax.ppermute(value, axis, pairs)  67 us
    reduce_scatter x1, waiting for transfers between devices, on_device(): lax.psum_scatter(combined.astype(jnp.bfloat16), 'tp', scatter_dimension=1...  39.7 us
    ppermute x7, waiting for transfers between devices, passed_along(): return lax.ppermute(value, axis, pairs)  33.2 us
    all_to_all x1, starting transfers between devices, on_device(): lax.all_to_all(outgoing[0], 'req', split_axis=0, concat_axis=2, tiled=True)  18.4 us
    all_to_all x1, starting transfers between devices, on_device(): lax.all_to_all(outgoing[2], 'req', split_axis=0, concat_axis=2, tiled=True)  17.3 us
    all_to_all x1, starting transfers between devices, on_device(): lax.all_to_all(outgoing[1], 'req', split_axis=0, concat_axis=2, tiled=True)  16.4 us
    all_to_all x1, starting transfers between devices, on_device(): lax.all_to_all(outbox, 'req', split_axis=0, concat_axis=0, tiled=True)  14.3 us
  transfers between devices with their start and end apart: 14, of which 7 were waited for; matrix products, arithmetic and copies ran while one was open for 17% of the time, Pallas kernels for 0%

commit v1 on v0

v1 whole, which is shorter than its diff:
```python
import jax
import jax.numpy as jnp
import numpy as np
from jax import lax
from jax.sharding import PartitionSpec as P


def passed_along(value, axis, steps):
    count = lax.axis_size(axis)
    pairs = [(source, (source + steps) % count) for source in range(count)]
    return lax.ppermute(value, axis, pairs)


def gathered_weight(weight):
    experts, rows, hidden = weight.shape
    flat = jnp.transpose(weight, (1, 0, 2)).reshape(rows, experts * hidden)
    return lax.all_gather(flat, "req", axis=0, tiled=True)


def on_device(
    tokens,
    attn_heads,
    out_proj,
    norm_gain,
    w_gate,
    w_up,
    w_down,
    routes,
    gate_weights,
    cache_pages,
    page_dest,
):
    tp_count = lax.axis_size("tp")
    tp_place = lax.axis_index("tp")
    tok_count, top_count = routes.shape
    experts, _, hidden = w_gate.shape
    model_width = tokens.shape[1]
    quarter_rows = tok_count // tp_count

    gate_full = gathered_weight(w_gate)
    up_full = gathered_weight(w_up)
    down_full = gathered_weight(w_down)

    partial_value = jnp.dot(attn_heads, out_proj, preferred_element_type=jnp.float32)
    partial_sent = partial_value.astype(jnp.bfloat16)

    def rows_of(value, block):
        return lax.dynamic_slice_in_dim(value, block * quarter_rows, quarter_rows, 0)

    attention = rows_of(partial_value, tp_place)
    for step in range(1, tp_count):
        outgoing = rows_of(partial_sent, (tp_place + step) % tp_count)
        attention = attention + passed_along(outgoing, "tp", step).astype(jnp.float32)
    residual = rows_of(tokens, tp_place).astype(jnp.float32) + attention
    inverse = lax.rsqrt(jnp.mean(residual * residual, axis=1, keepdims=True) + 1e-05)
    normed_own = (residual * inverse * norm_gain).astype(jnp.bfloat16)
    normed = jnp.zeros((tok_count, model_width), jnp.bfloat16)
    normed = lax.dynamic_update_slice_in_dim(normed, normed_own, tp_place * quarter_rows, 0)
    for step in range(1, tp_count):
        block = (tp_place - step) % tp_count
        normed = lax.dynamic_update_slice_in_dim(
            normed, passed_along(normed_own, "tp", step), block * quarter_rows, 0
        )

    expert_ids = jnp.arange(experts, dtype=jnp.int32)
    factor = jnp.sum(
        jnp.where(routes[:, :, None] == expert_ids, gate_weights[:, :, None], 0.0), axis=1
    )
    factor_wide = jnp.broadcast_to(
        factor[:, :, None], (tok_count, experts, hidden)
    ).reshape(tok_count, experts * hidden)

    pre_gate = jnp.dot(normed, gate_full, preferred_element_type=jnp.float32)
    pre_up = jnp.dot(normed, up_full, preferred_element_type=jnp.float32)
    active = (factor_wide * (jax.nn.silu(pre_gate) * pre_up)).astype(jnp.bfloat16)
    combined = lax.dot_general(
        active, down_full, (((1,), (1,)), ((), ())), preferred_element_type=jnp.float32
    )
    own_rows = rows_of(combined, tp_place) + residual
    combined = lax.dynamic_update_slice_in_dim(combined, own_rows, tp_place * quarter_rows, 0)
    layer_output = lax.psum_scatter(
        combined.astype(jnp.bfloat16), "tp", scatter_dimension=1, tiled=True
    )

    spread = cache_pages.shape[0]
    page_offsets = page_dest % spread
    page_order = (
        jnp.zeros((spread,), jnp.int32).at[page_offsets].set(jnp.arange(spread, dtype=jnp.int32))
    )
    ranked = cache_pages[page_order]
    arrived_pages = [ranked[0]]
    for offset in range(1, spread):
        arrived_pages.append(passed_along(ranked[offset], "req", offset))
    decode_cache = jnp.stack(arrived_pages)
    return (layer_output, decode_cache)


def solution(mesh):
    in_specs = (
        P("req", None),
        P("req", "tp"),
        P("tp", None),
        P(),
        P(None, "req", "tp"),
        P(None, "req", "tp"),
        P(None, "req", "tp"),
        P("req", None),
        P("req", None),
        P("req", None, "tp", None),
        P("req"),
    )
    out_specs = (P("req", "tp"), P("req", None, "tp", None))
    return jax.shard_map(
        on_device, mesh=mesh, in_specs=in_specs, out_specs=out_specs, check_vma=False
    )
```

time: 439 us -> 328 us (0.75)
  starting transfers between devices: 142 us -> 53.2 us
  local copies, waits for them, and re-layouts: 63.4 us -> 12.7 us
  waiting for transfers between devices: 187 us -> 226 us
  other arithmetic: 13 us -> 2.57 us
    all_gather x0 -> x3, waiting for transfers between devices: none -> 206 us  [gathered_weight(): return lax.all_gather(flat, 'req', axis=0, tiled=True)]
    all_to_all x5 -> x0, waiting for transfers between devices: 103 us -> none  [the longest x1 94.2 us: on_device(): lax.all_to_all(outbox, 'req', split_axis=0, concat_axis=0, tiled=True)]
    all_to_all x5 -> x0, starting transfers between devices: 74.7 us -> none  [the longest x1 18.4 us: on_device(): lax.all_to_all(outgoing[0], 'req', split_axis=0, concat_axis=2, tiled=True)]
    gather x11 -> x0, local copies, waits for them, and re-layouts: 31.5 us -> none  [the longest x2 11.9 us: on_device(): normed[slot_token] * slot_live[:, None]]
    ppermute x7 -> x13, waiting for transfers between devices: 33.2 us -> 2.28 us  [passed_along(): return lax.ppermute(value, axis, pairs)]
    reduce_scatter x1, waiting for transfers between devices: 39.7 us -> 15.5 us  [on_device(): lax.psum_scatter(combined.astype(jnp.bfloat16), 'tp', scatter_dimension=1...]
    ppermute x7 -> x13, starting transfers between devices: 67 us -> 53 us  [passed_along(): return lax.ppermute(value, axis, pairs)]
    scatter x2 -> x0, local copies, waits for them, and re-layouts: 11.9 us -> none  [the longest x1 7.59 us: on_device(): slot_live = jnp.zeros((slot_total,), jnp.bfloat16).at[flat_slots].set(1.0)]
  transfers between devices with their start and end apart: 14 -> 17, of which waited for: 7 -> 6; matrix products, arithmetic and copies ran while one was open for 17% -> 10% of each run, Pallas kernels for 0% -> 0%
where the time goes in v1:
time: 328 us; the launch traced here: 326 us
  waiting for transfers between devices  226 us (69%)
  starting transfers between devices  53.2 us (16%)
  matrix products  17.3 us (5%)
  between operations  14.2 us (4%)
  local copies, waits for them, and re-layouts  12.7 us (4%)
    all_gather x3, waiting for transfers between devices, gathered_weight(): return lax.all_gather(flat, 'req', axis=0, tiled=True)  206 us
    ppermute x13, starting transfers between devices, passed_along(): return lax.ppermute(value, axis, pairs)  53 us
    reduce_scatter x1, waiting for transfers between devices, on_device(): lax.psum_scatter(combined.astype(jnp.bfloat16), 'tp', scatter_dimension=1...  15.5 us
    dot_general x1, matrix products, on_device(): lax.dot_general(active, down_full, (((1,), (1,)), ((), ())), preferred_el...  11.6 us
  transfers between devices with their start and end apart: 17, of which 6 were waited for; matrix products, arithmetic and copies ran while one was open for 10% of the time, Pallas kernels for 0%

profile of v1, /device:TPU:1, one launch (start us, length us, event | category | flops | bytes accessed | tf_op | source)
XLA Modules:
  0.0 326.0 jit_solution(7272993079808292789)
XLA Ops:
  10.6 3.9 %collective-permute-start = (bf16[32,1024]{1,0:T(8,128)(2,1)S(1)}, bf16[32,1024]{1,0:T(8,128)(2,1)S(1)}, u32[]{:S(2)}, u32[]{:S(2)}) collective-permute-start(bf16[32,1024]{1,0:T(8,128)(2,1)S(1)} %get-tuple-element.14), channel_id=1, source_target_pairs={{0,1},{1,2},{2,3},{3,0},{4,5},{5,6},{6,7},{7,4},{8,9},{9,10},{10,1... | collective-permute-start | bytes 196616 | tf_op jit(solution)/shard_map/ppermute | solution.py:11
  14.6 4.4 %collective-permute-start.1 = (bf16[32,1024]{1,0:T(8,128)(2,1)S(1)}, bf16[32,1024]{1,0:T(8,128)(2,1)S(1)}, u32[]{:S(2)}, u32[]{:S(2)}) collective-permute-start(bf16[32,1024]{1,0:T(8,128)(2,1)S(1)} %get-tuple-element.16), channel_id=1, source_target_pairs={{0,2},{1,3},{2,0},{3,1},{4,6},{5,7},{6,4},{7,5},{8,10},{9,11},{10,... | collective-permute-start | bytes 196616 | tf_op jit(solution)/shard_map/ppermute | solution.py:11
  19.0 3.1 collective-permute-start.2
  23.3 1.6 gather_fusion
  26.0 5.4 %collective-permute-start.6 = (bf16[128,2,128]{2,1,0:T(2,128)(2,1)S(1)}, bf16[128,2,128]{2,1,0:T(2,128)(2,1)S(1)}, u32[]{:S(2)}, u32[]{:S(2)}) collective-permute-start(bf16[128,2,128]{2,1,0:T(2,128)(2,1)S(1)} %get-tuple-element.12), channel_id=1, source_target_pairs={{0,4},{4,8},{8,12},{12,16},{16,20},{20,24},{24,28},{28,32},{32,36}... | collective-permute-start | bytes 196616 | tf_op jit(solution)/shard_map/ppermute | solution.py:11
  31.4 4.0 %collective-permute-start.7 = (bf16[128,2,128]{2,1,0:T(2,128)(2,1)S(1)}, bf16[128,2,128]{2,1,0:T(2,128)(2,1)S(1)}, u32[]{:S(2)}, u32[]{:S(2)}) collective-permute-start(bf16[128,2,128]{2,1,0:T(2,128)(2,1)S(1)} %get-tuple-element.11), channel_id=1, source_target_pairs={{0,8},{4,12},{8,16},{12,20},{16,24},{20,28},{24,32},{28,36},{32,40... | collective-permute-start | bytes 196616 | tf_op jit(solution)/shard_map/ppermute | solution.py:11
  35.6 4.0 %collective-permute-start.8 = (bf16[128,2,128]{2,1,0:T(2,128)(2,1)S(1)}, bf16[128,2,128]{2,1,0:T(2,128)(2,1)S(1)}, u32[]{:S(2)}, u32[]{:S(2)}) collective-permute-start(bf16[128,2,128]{2,1,0:T(2,128)(2,1)S(1)} %get-tuple-element.10), channel_id=1, source_target_pairs={{0,12},{4,16},{8,20},{12,24},{16,28},{20,32},{24,36},{28,40},{32,4... | collective-permute-start | bytes 196616 | tf_op jit(solution)/shard_map/ppermute | solution.py:11
  39.6 6.1 %collective-permute-start.9 = (bf16[128,2,128]{2,1,0:T(2,128)(2,1)S(1)}, bf16[128,2,128]{2,1,0:T(2,128)(2,1)S(1)}, u32[]{:S(2)}, u32[]{:S(2)}) collective-permute-start(bf16[128,2,128]{2,1,0:T(2,128)(2,1)S(1)} %get-tuple-element.9), channel_id=1, source_target_pairs={{0,16},{4,20},{8,24},{12,28},{16,32},{20,36},{24,40},{28,44},{32,4... | collective-permute-start | bytes 196616 | tf_op jit(solution)/shard_map/ppermute | solution.py:11
  45.8 4.3 %collective-permute-start.10 = (bf16[128,2,128]{2,1,0:T(2,128)(2,1)}, bf16[128,2,128]{2,1,0:T(2,128)(2,1)}, u32[]{:S(2)}, u32[]{:S(2)}) collective-permute-start(bf16[128,2,128]{2,1,0:T(2,128)(2,1)} %get-tuple-element.8), channel_id=1, source_target_pairs={{0,20},{4,24},{8,28},{12,32},{16,36},{20,40},{24,44},{28,48},{32,5... | collective-permute-start | bytes 196616 | tf_op jit(solution)/shard_map/ppermute | solution.py:11
  51.2 2.5 collective-permute-start.11
  54.5 7.0 %collective-permute-start.12 = (bf16[128,2,128]{2,1,0:T(2,128)(2,1)}, bf16[128,2,128]{2,1,0:T(2,128)(2,1)}, u32[]{:S(2)}, u32[]{:S(2)}) collective-permute-start(bf16[128,2,128]{2,1,0:T(2,128)(2,1)} %get-tuple-element.6), channel_id=1, source_target_pairs={{0,28},{4,32},{8,36},{12,40},{16,44},{20,48},{24,52},{28,56},{32,6... | collective-permute-start | bytes 196616 | tf_op jit(solution)/shard_map/ppermute | solution.py:11
  62.2 2.2 collective-permute-start.3
  65.1 2.5 collective-permute-start.4
  68.4 3.6 %collective-permute-start.5 = (bf16[32,1024]{1,0:T(8,128)(2,1)S(1)}, bf16[32,1024]{1,0:T(8,128)(2,1)S(1)}, u32[]{:S(2)}, u32[]{:S(2)}) collective-permute-start(bf16[32,1024]{1,0:T(8,128)(2,1)S(1)} %get-tuple-element.3), channel_id=1, source_target_pairs={{0,3},{1,0},{2,1},{3,2},{4,7},{5,4},{6,5},{7,6},{8,11},{9,8},{10,9... | collective-permute-start | bytes 196616 | tf_op jit(solution)/shard_map/ppermute | solution.py:11
  72.0 2.1 collective-permute-done.5
  74.2 34.8 %all-gather.4.cloned.1.call-done = bf16[1024,4096]{1,0:T(8,128)(2,1)} async-done(((bf16[8,4096]{1,0:T(8,128)(2,1)}), bf16[1024,4096]{1,0:T(8,128)(2,1)}) %all-gather.4.cloned.1.call-update) | async-done | bytes 8388624 | tf_op jit(solution)/shard_map/all_gather | solution.py:17
  109.0 4.6 %fusion.11 = f32[128,4096]{1,0:T(8,128)S(1)} fusion(bf16[128,1024]{1,0:T(8,128)(2,1)S(1)} %constant_dynamic-update-slice_fusion, bf16[1024,4096]{1,0:T(8,128)(2,1)} %all-gather.4.cloned.1.call-done), kind=kOutput, calls=%fused_computation.47 | convolution fusion | flops 1073741824 | bytes 10747904 | tf_op jit(solution)/shard_map/dot_general | solution.py:73
  113.6 83.3 %all-gather.6.cloned.1.call-done = bf16[1024,4096]{1,0:T(8,128)(2,1)} async-done(((bf16[8,4096]{1,0:T(8,128)(2,1)}), bf16[1024,4096]{1,0:T(8,128)(2,1)}) %all-gather.6.cloned.1.call-update) | async-done | bytes 8388624 | tf_op jit(solution)/shard_map/all_gather | solution.py:17
  197.0 88.0 %all-gather.8.cloned.1.call-done = bf16[1024,4096]{1,0:T(8,128)(2,1)} async-done(((bf16[8,4096]{1,0:T(8,128)(2,1)}), bf16[1024,4096]{1,0:T(8,128)(2,1)}) %all-gather.8.cloned.1.call-update) | async-done | bytes 8388624 | tf_op jit(solution)/shard_map/all_gather | solution.py:17
  284.9 1.9 broadcast_in_dim.34
  286.9 11.6 %fusion.1 = f32[128,1024]{1,0:T(8,128)S(1)} fusion(bf16[1024,4096]{1,0:T(8,128)(2,1)} %all-gather.8.cloned.1.call-done, f32[16,8,32,128]{3,2,1,0:T(8,128)} %bitcast.50, f32[128,4096]{1,0:T(8,128)S(1)} %fusion.11, bf16[128,1024]{1,0:T(8,128)(2,1)S(1)} %constant_dynamic-update-slice_fusion, bf16[1024,4096]{1,0:T(8,128)(2,1)} %all-gather.6.cloned.1.call-done), kind=kOutput, calls=%fused_computation.4 | convolution fusion | flops 2151153664 | bytes 21757952 | tf_op jit(solution)/shard_map/dot_general | solution.py:76
  299.3 1.5 bitcast_dynamic-update-slice_fusion.2
  300.9 1.5 bitcast_dynamic-update-slice_fusion.1
  303.9 15.5 %reduce-scatter.2.cloned.1.call-done = bf16[128,256]{1,0:T(8,128)(2,1)} async-done(((bf16[128,1024]{1,0:T(8,128)(2,1)}), bf16[128,256]{1,0:T(8,128)(2,1)}) %reduce-scatter.2.cloned.1.call-update) | async-done | bytes 65552 | tf_op jit(solution)/shard_map/reduce_scatter | solution.py:81
  (54 shorter events, 12.1 us)
Async XLA Ops:
  7.2 2.3 copy-start
  7.2 16.1 %copy-start.1 = (bf16[8,128,2,128]{3,2,1,0:T(2,128)(2,1)S(1)}, bf16[8,128,2,128]{3,2,1,0:T(2,128)(2,1)}, u32[]{:S(2)}) copy-start(bf16[8,128,2,128]{3,2,1,0:T(2,128)(2,1)} %param.20) | copy-start | bytes 1572868
  7.2 101.8 %all-gather.4.cloned.1.call-start = ((), (), s32[]{:S(2)}) async-start(), calls=%async_computation.1 | async-start | bytes 8454144 | tf_op jit(solution)/shard_map/all_gather | solution.py:17
  7.9 189.0 %all-gather.6.cloned.1.call-start = ((), (), s32[]{:S(2)}) async-start(), calls=%async_computation.2 | async-start | bytes 8454144 | tf_op jit(solution)/shard_map/all_gather | solution.py:17
  8.0 27.5 %copy-start.3 = (f32[128,8]{0,1:T(8,128)S(1)}, f32[128,8]{0,1:T(8,128)}, u32[]{:S(2)}) copy-start(f32[128,8]{0,1:T(8,128)} %param.19) | copy-start | bytes 12292
  8.0 27.5 %copy-start.4 = (s32[128,8]{0,1:T(8,128)S(1)}, s32[128,8]{0,1:T(8,128)}, u32[]{:S(2)}) copy-start(s32[128,8]{0,1:T(8,128)} %param.18) | copy-start | bytes 12292
  8.7 276.3 %all-gather.8.cloned.1.call-start = ((), (), s32[]{:S(2)}) async-start(), calls=%async_computation.3 | async-start | bytes 8454144 | tf_op jit(solution)/shard_map/all_gather | solution.py:17
  9.4 310.0 %reduce-scatter.2.cloned.1.call-start = ((), (), s32[]{:S(2)}) async-start(), calls=%async_computation.4 | async-start | bytes 327680 | tf_op jit(solution)/shard_map/reduce_scatter | solution.py:81
  10.6 40.5 %copy-start.2 = (f32[1024]{0:T(1024)S(1)}, f32[1024]{0:T(1024)}, u32[]{:S(2)}) copy-start(f32[1024]{0:T(1024)} %param.14) | copy-start | bytes 12292
  10.6 25.0 %collective-permute-start = (bf16[32,1024]{1,0:T(8,128)(2,1)S(1)}, bf16[32,1024]{1,0:T(8,128)(2,1)S(1)}, u32[]{:S(2)}, u32[]{:S(2)}) collective-permute-start(bf16[32,1024]{1,0:T(8,128)(2,1)S(1)} %get-tuple-element.14), channel_id=1, source_target_pairs={{0,1},{1,2},{2,3},{3,0},{4,5},{5,6},{6,7},{7,4},{8,9},{9,10},{10,1... | collective-permute-start | bytes 196616 | tf_op jit(solution)/shard_map/ppermute | solution.py:11
  14.6 25.0 %collective-permute-start.1 = (bf16[32,1024]{1,0:T(8,128)(2,1)S(1)}, bf16[32,1024]{1,0:T(8,128)(2,1)S(1)}, u32[]{:S(2)}, u32[]{:S(2)}) collective-permute-start(bf16[32,1024]{1,0:T(8,128)(2,1)S(1)} %get-tuple-element.16), channel_id=1, source_target_pairs={{0,2},{1,3},{2,0},{3,1},{4,6},{5,7},{6,4},{7,5},{8,10},{9,11},{10,... | collective-permute-start | bytes 196616 | tf_op jit(solution)/shard_map/ppermute | solution.py:11
  19.0 26.8 %collective-permute-start.2 = (bf16[32,1024]{1,0:T(8,128)(2,1)S(1)}, bf16[32,1024]{1,0:T(8,128)(2,1)S(1)}, u32[]{:S(2)}, u32[]{:S(2)}) collective-permute-start(bf16[32,1024]{1,0:T(8,128)(2,1)S(1)} %get-tuple-element.15), channel_id=1, source_target_pairs={{0,3},{1,0},{2,1},{3,2},{4,7},{5,4},{6,5},{7,6},{8,11},{9,8},{10,9... | collective-permute-start | bytes 196616 | tf_op jit(solution)/shard_map/ppermute | solution.py:11
  26.0 25.3 %collective-permute-start.6 = (bf16[128,2,128]{2,1,0:T(2,128)(2,1)S(1)}, bf16[128,2,128]{2,1,0:T(2,128)(2,1)S(1)}, u32[]{:S(2)}, u32[]{:S(2)}) collective-permute-start(bf16[128,2,128]{2,1,0:T(2,128)(2,1)S(1)} %get-tuple-element.12), channel_id=1, source_target_pairs={{0,4},{4,8},{8,12},{12,16},{16,20},{20,24},{24,28},{28,32},{32,36}... | collective-permute-start | bytes 196616 | tf_op jit(solution)/shard_map/ppermute | solution.py:11
  31.4 23.1 %collective-permute-start.7 = (bf16[128,2,128]{2,1,0:T(2,128)(2,1)S(1)}, bf16[128,2,128]{2,1,0:T(2,128)(2,1)S(1)}, u32[]{:S(2)}, u32[]{:S(2)}) collective-permute-start(bf16[128,2,128]{2,1,0:T(2,128)(2,1)S(1)} %get-tuple-element.11), channel_id=1, source_target_pairs={{0,8},{4,12},{8,16},{12,20},{16,24},{20,28},{24,32},{28,36},{32,40... | collective-permute-start | bytes 196616 | tf_op jit(solution)/shard_map/ppermute | solution.py:11
  35.6 26.6 %collective-permute-start.8 = (bf16[128,2,128]{2,1,0:T(2,128)(2,1)S(1)}, bf16[128,2,128]{2,1,0:T(2,128)(2,1)S(1)}, u32[]{:S(2)}, u32[]{:S(2)}) collective-permute-start(bf16[128,2,128]{2,1,0:T(2,128)(2,1)S(1)} %get-tuple-element.10), channel_id=1, source_target_pairs={{0,12},{4,16},{8,20},{12,24},{16,28},{20,32},{24,36},{28,40},{32,4... | collective-permute-start | bytes 196616 | tf_op jit(solution)/shard_map/ppermute | solution.py:11
  39.6 25.4 %collective-permute-start.9 = (bf16[128,2,128]{2,1,0:T(2,128)(2,1)S(1)}, bf16[128,2,128]{2,1,0:T(2,128)(2,1)S(1)}, u32[]{:S(2)}, u32[]{:S(2)}) collective-permute-start(bf16[128,2,128]{2,1,0:T(2,128)(2,1)S(1)} %get-tuple-element.9), channel_id=1, source_target_pairs={{0,16},{4,20},{8,24},{12,28},{16,32},{20,36},{24,40},{28,44},{32,4... | collective-permute-start | bytes 196616 | tf_op jit(solution)/shard_map/ppermute | solution.py:11
  45.8 253.5 %collective-permute-start.10 = (bf16[128,2,128]{2,1,0:T(2,128)(2,1)}, bf16[128,2,128]{2,1,0:T(2,128)(2,1)}, u32[]{:S(2)}, u32[]{:S(2)}) collective-permute-start(bf16[128,2,128]{2,1,0:T(2,128)(2,1)} %get-tuple-element.8), channel_id=1, source_target_pairs={{0,20},{4,24},{8,28},{12,32},{16,36},{20,40},{24,44},{28,48},{32,5... | collective-permute-start | bytes 196616 | tf_op jit(solution)/shard_map/ppermute | solution.py:11
  51.2 249.6 %collective-permute-start.11 = (bf16[128,2,128]{2,1,0:T(2,128)(2,1)}, bf16[128,2,128]{2,1,0:T(2,128)(2,1)}, u32[]{:S(2)}, u32[]{:S(2)}) collective-permute-start(bf16[128,2,128]{2,1,0:T(2,128)(2,1)} %get-tuple-element.7), channel_id=1, source_target_pairs={{0,24},{4,28},{8,32},{12,36},{16,40},{20,44},{24,48},{28,52},{32,5... | collective-permute-start | bytes 196616 | tf_op jit(solution)/shard_map/ppermute | solution.py:11
  54.5 247.9 %collective-permute-start.12 = (bf16[128,2,128]{2,1,0:T(2,128)(2,1)}, bf16[128,2,128]{2,1,0:T(2,128)(2,1)}, u32[]{:S(2)}, u32[]{:S(2)}) collective-permute-start(bf16[128,2,128]{2,1,0:T(2,128)(2,1)} %get-tuple-element.6), channel_id=1, source_target_pairs={{0,28},{4,32},{8,36},{12,40},{16,44},{20,48},{24,52},{28,56},{32,6... | collective-permute-start | bytes 196616 | tf_op jit(solution)/shard_map/ppermute | solution.py:11
  62.2 6.2 %collective-permute-start.3 = (bf16[32,1024]{1,0:T(8,128)(2,1)S(1)}, bf16[32,1024]{1,0:T(8,128)(2,1)S(1)}, u32[]{:S(2)}, u32[]{:S(2)}) collective-permute-start(bf16[32,1024]{1,0:T(8,128)(2,1)S(1)} %get-tuple-element.3), channel_id=1, source_target_pairs={{0,1},{1,2},{2,3},{3,0},{4,5},{5,6},{6,7},{7,4},{8,9},{9,10},{10,1... | collective-permute-start | bytes 196616 | tf_op jit(solution)/shard_map/ppermute | solution.py:11
  65.1 6.9 %collective-permute-start.4 = (bf16[32,1024]{1,0:T(8,128)(2,1)S(1)}, bf16[32,1024]{1,0:T(8,128)(2,1)S(1)}, u32[]{:S(2)}, u32[]{:S(2)}) collective-permute-start(bf16[32,1024]{1,0:T(8,128)(2,1)S(1)} %get-tuple-element.3), channel_id=1, source_target_pairs={{0,2},{1,3},{2,0},{3,1},{4,6},{5,7},{6,4},{7,5},{8,10},{9,11},{10,... | collective-permute-start | bytes 196616 | tf_op jit(solution)/shard_map/ppermute | solution.py:11
  68.4 5.8 %collective-permute-start.5 = (bf16[32,1024]{1,0:T(8,128)(2,1)S(1)}, bf16[32,1024]{1,0:T(8,128)(2,1)S(1)}, u32[]{:S(2)}, u32[]{:S(2)}) collective-permute-start(bf16[32,1024]{1,0:T(8,128)(2,1)S(1)} %get-tuple-element.3), channel_id=1, source_target_pairs={{0,3},{1,0},{2,1},{3,2},{4,7},{5,4},{6,5},{7,6},{8,11},{9,8},{10,9... | collective-permute-start | bytes 196616 | tf_op jit(solution)/shard_map/ppermute | solution.py:11
Sparse Core Ops, SparseCore 0:
  11.2 97.7 all-gather.3
  112.1 84.8 all-gather.5
  200.1 84.8 all-gather.7
  299.4 19.9 reduce-scatter.1

commit v2 on v1

v2 whole, which is shorter than its diff:
```python
import functools

import jax
import jax.numpy as jnp
from jax import lax
from jax.experimental import pallas as pl
from jax.experimental.pallas import tpu as pltpu
from jax.sharding import PartitionSpec as P

MESH = pl.DeviceIdType.MESH
RING = 8
CORES = 2
STREAMS = 4
LAST = RING - 1
F32 = jnp.float32
BF16 = jnp.bfloat16


def expert_kernel(
    req_count,
    tp_count,
    part_ref,
    tokens_ref,
    factor_ref,
    gain_ref,
    gate_ref,
    up_ref,
    down_ref,
    pages_ref,
    out_ref,
    cache_ref,
    full,
    parts,
    both,
    factors,
    normed,
    residual,
    active,
    outbox,
    inbox,
    local_sem,
    swap_sem,
    part_sem,
    page_sem,
    first_sem,
    second_sem,
    back_sem,
):
    peers = tp_count * CORES
    me = lax.axis_index("req")
    tp = lax.axis_index("tp")
    core = lax.rem(me, CORES)
    z = lax.rem(me // CORES, RING)
    y = me // (CORES * RING)
    mine = tp * CORES + core
    other = 1 - core
    chip = me - core
    tok_count, width = tokens_ref.shape
    half = full.shape[4]
    cut = half // STREAMS
    pages = pages_ref.shape[0]
    share = width // tp_count

    def at(y_place, z_place, core_place):
        return (y_place * RING + z_place) * CORES + core_place

    def peer(index):
        return (chip + lax.rem(index, CORES), index // CORES)

    ahead_y = (at(lax.rem(y + 1, RING), z, core), tp)
    behind_y = (at(lax.rem(y + LAST, RING), z, core), tp)
    ahead_z = (at(y, lax.rem(z + 1, RING), core), tp)
    behind_z = (at(y, lax.rem(z + LAST, RING), core), tp)
    partner = (chip + other, tp)

    barrier = pltpu.get_barrier_semaphore()

    def greet(device):
        pl.semaphore_signal(barrier, inc=1, device_id=device, device_id_type=MESH)

    for device in (ahead_y, behind_y, ahead_z, behind_z):
        greet(device)
    for step in range(1, peers):
        greet(peer(lax.rem(mine + step, peers)))
    for step in range(1, pages):
        greet((lax.rem(me + step, req_count), tp))
        greet((lax.rem(me + req_count - step, req_count), tp))
    pl.semaphore_wait(barrier, 4 + peers - 1 + 2 * (pages - 1))

    def remote(source, target, sems, device):
        return pltpu.make_async_remote_copy(
            src_ref=source,
            dst_ref=target,
            send_sem=sems.at[0],
            recv_sem=sems.at[1],
            device_id=device,
            device_id_type=MESH,
        )

    rows = pl.ds(pl.multiple_of(core * 8, 8), 8)
    kept = pl.ds(pl.multiple_of(core * half, half), half)
    given = pl.ds(pl.multiple_of(other * half, half), half)
    swaps, locals_ = [], []
    for index, weight in enumerate((gate_ref, up_ref, down_ref)):
        place = full.at[index, y, z, rows, :]
        swaps.append(remote(weight.at[:, given], place, swap_sem.at[index], partner))
        locals_.append(pltpu.make_async_copy(weight.at[:, kept], place, local_sem.at[index]))
    swaps.append(remote(tokens_ref, both.at[core], swap_sem.at[3], partner))
    swaps.append(remote(factor_ref.at[other], factors.at[core], swap_sem.at[4], partner))
    locals_.append(pltpu.make_async_copy(tokens_ref, both.at[core], local_sem.at[3]))
    locals_.append(pltpu.make_async_copy(factor_ref.at[core], factors.at[core], local_sem.at[4]))
    locals_.append(pltpu.make_async_copy(part_ref, parts.at[mine], local_sem.at[5]))
    locals_.append(pltpu.make_async_copy(pages_ref.at[0], cache_ref.at[0], local_sem.at[6]))
    for copy in swaps + locals_:
        copy.start()

    def page_copy(step):
        device = (lax.rem(me + step, req_count), tp)
        return remote(pages_ref.at[step], cache_ref.at[step], page_sem.at[step], device)

    def part_copy(step):
        device = peer(lax.rem(mine + step, peers))
        return remote(part_ref, parts.at[mine], part_sem.at[step], device)

    for step in range(1, peers):
        part_copy(step).start()
    for step in range(pages - 1, 0, -1):
        page_copy(step).start()
    for index in range(3):
        swaps[index].wait_recv()
        locals_[index].wait()

    def back(place, step):
        return lax.rem(place + RING - step, RING)

    def forth(place, step):
        return lax.rem(place + step, RING)

    def first_copy(stream, step):
        columns = pl.ds(stream * cut, cut)
        y_place, z_place = (
            (back(y, step), z),
            (forth(y, step), z),
            (y, back(z, step)),
            (y, forth(z, step)),
        )[stream]
        device = (ahead_y, behind_y, ahead_z, behind_z)[stream]
        block = full.at[:, y_place, z_place, :, columns]
        return remote(block, block, first_sem.at[stream, step], device)

    def second_copy(piece, stream, step):
        weight = min(piece, 2)
        size = cut if piece < 2 else cut // 2
        columns = pl.ds(stream * cut + max(piece - 2, 0) * size, size)
        device = (ahead_z, behind_z, ahead_y, behind_y)[stream]
        if stream == 0:
            block = full.at[weight, :, back(z, step), :, columns]
        elif stream == 1:
            block = full.at[weight, :, forth(z, step), :, columns]
        elif stream == 2:
            block = full.at[weight, back(y, step), :, :, columns]
        else:
            block = full.at[weight, forth(y, step), :, :, columns]
        return remote(block, block, second_sem.at[piece, stream, step], device)

    def first_step(step, carry):
        for stream in range(STREAMS):
            first_copy(stream, step).start()
        for stream in range(STREAMS):
            first_copy(stream, step).wait_recv()
        return carry

    lax.fori_loop(0, LAST, first_step, 0)

    for piece in (0, 1):
        for stream in range(STREAMS):
            second_copy(piece, stream, 0).start()

    def second_step(pieces, step):
        for piece in pieces:
            for stream in range(STREAMS):
                second_copy(piece, stream, step - 1).wait_recv()
                second_copy(piece, stream, step).start()

    second_step((0, 1), 1)

    for step in range(1, peers):
        part_copy(step).wait_recv()
    for index in (3, 4):
        swaps[index].wait_recv()
    for index in (3, 4, 5):
        locals_[index].wait()
    lines = 32

    def norm_step(step, carry):
        which = step // (tok_count // lines)
        start = pl.multiple_of(lax.rem(step, tok_count // lines) * lines, lines)
        span = pl.ds(start, lines)
        total = both[which, span, :].astype(F32)
        for place in range(tp_count):
            total = total + parts[place * CORES + which, span, :].astype(F32)
        residual[which, span, :] = total
        inverse = lax.rsqrt(jnp.mean(total * total, axis=1, keepdims=True) + 1e-05)
        normed[which, span, :] = (total * inverse * gain_ref[...]).astype(BF16)
        return carry

    lax.fori_loop(0, CORES * tok_count // lines, norm_step, 0)

    def gate_up_step(step, carry):
        second_step((0, 1), step)
        return carry

    lax.fori_loop(2, LAST, gate_up_step, 0)
    for piece in (2, 3):
        for stream in range(STREAMS):
            second_copy(piece, stream, 0).start()
    for piece in (0, 1):
        for stream in range(STREAMS):
            second_copy(piece, stream, LAST - 1).wait_recv()

    chunk = half // RING
    hidden = 128
    all_rows = CORES * tok_count

    def expert_part(index):
        columns = pl.ds(pl.multiple_of(index * chunk, chunk), chunk)
        lhs = normed[...].reshape(all_rows, width)
        pre_gate = jnp.dot(
            lhs, full[0, :, :, :, columns].reshape(width, chunk), preferred_element_type=F32
        )
        pre_up = jnp.dot(
            lhs, full[1, :, :, :, columns].reshape(width, chunk), preferred_element_type=F32
        )
        value = pre_gate / (1.0 + jnp.exp(-pre_gate)) * pre_up
        table = factors[...].reshape(all_rows, 128)
        lanes = lax.broadcasted_iota(jnp.int32, table.shape, 1)
        for expert in range(chunk // hidden):
            picked = jnp.where(lanes == index * (chunk // hidden) + expert, table, 0.0)
            weight = jnp.sum(picked, axis=1, keepdims=True)
            scaled = value[:, expert * hidden : (expert + 1) * hidden] * weight
            spot = pl.ds(pl.multiple_of(index * chunk + expert * hidden, hidden), hidden)
            active[:, spot] = scaled.astype(BF16)

    expert_part(0)

    def down_step(step, carry):
        second_step((2, 3), step)
        expert_part(step)
        return carry

    lax.fori_loop(1, LAST, down_step, 0)
    expert_part(LAST)
    for piece in (2, 3):
        for stream in range(STREAMS):
            second_copy(piece, stream, LAST - 1).wait_recv()

    def back_copy(place, which):
        index = place * CORES + which
        step = lax.rem(index + peers - mine, peers)
        return remote(
            outbox.at[place, which],
            inbox.at[mine],
            back_sem.at[step],
            (chip + which, place),
        )

    height = RING // tp_count

    def down_part(place):
        block = full[2, pl.ds(place * height, height)].reshape(share, half)
        return lax.dot_general(
            active[...], block, (((1,), (1,)), ((), ())), preferred_element_type=F32
        )

    def down_turn(step, carry):
        place = lax.rem(tp + step, tp_count)
        value = down_part(place)
        outbox[place] = value.astype(BF16).reshape(CORES, tok_count, share)
        return carry

    for step in range(1, tp_count):
        down_turn(step, 0)
        if step > 1:
            place = lax.rem(tp + step - 1, tp_count)
            for which in range(CORES):
                back_copy(place, which).start()
    down_turn(0, 0)
    place = lax.rem(tp + tp_count - 1, tp_count)
    for which in range(CORES):
        back_copy(place, which).start()
    back_copy(tp, other).start()

    columns = pl.ds(pl.multiple_of(tp * share, share), share)
    total = residual[core, :, columns] + outbox[tp, core].astype(F32)

    def came(step):
        return remote(outbox.at[tp, other], inbox.at[mine], back_sem.at[step], partner)

    for step in range(1, peers):
        came(step).wait_recv()
        source = lax.rem(mine + peers - step, peers)
        total = total + inbox[source].astype(F32)
    out_ref[...] = total.astype(out_ref.dtype)

    for step in range(1, peers):
        came(step).wait_send()
        part_copy(step).wait_send()
    for copy in swaps:
        copy.wait_send()
    locals_[6].wait()
    for step in range(1, pages):
        page_copy(step).wait()

    def drain(step, carry):
        for stream in range(STREAMS):
            first_copy(stream, step).wait_send()
            for piece in range(4):
                second_copy(piece, stream, step).wait_send()
        return carry

    lax.fori_loop(0, LAST, drain, 0)


def on_device(
    tokens,
    attn_heads,
    out_proj,
    norm_gain,
    w_gate,
    w_up,
    w_down,
    routes,
    gate_weights,
    cache_pages,
    page_dest,
):
    req_count = lax.axis_size("req")
    tp_count = lax.axis_size("tp")
    tok_count, top_count = routes.shape
    experts, rows, hidden = w_gate.shape
    width = tokens.shape[1]
    half = experts * hidden // CORES

    def flat(weight):
        return jnp.transpose(weight, (1, 0, 2)).reshape(rows, experts * hidden)

    part = jnp.dot(attn_heads, out_proj, preferred_element_type=F32).astype(BF16)

    lanes = jnp.arange(128, dtype=jnp.int32)
    own = experts // CORES
    ids = jnp.stack([jnp.where(lanes < own, lanes + h * own, -1) for h in range(CORES)])
    factor = jnp.zeros((CORES, tok_count, 128), F32)
    for route in range(top_count):
        factor = factor + jnp.where(
            routes[None, :, route, None] == ids[:, None, :], gate_weights[None, :, route, None], 0.0
        )

    spread = cache_pages.shape[0]
    places = jnp.arange(spread, dtype=jnp.int32)
    page_order = jnp.sum(
        jnp.where((page_dest % spread)[None, :] == places[:, None], places[None, :], 0), axis=1
    )
    ranked = cache_pages[page_order]

    vmem = pl.BlockSpec(memory_space=pltpu.VMEM)
    anywhere = pl.BlockSpec(memory_space=pl.ANY)
    peers = tp_count * CORES
    share = width // tp_count
    dma = pltpu.SemaphoreType.DMA
    return pl.pallas_call(
        functools.partial(expert_kernel, req_count, tp_count),
        out_shape=(
            jax.ShapeDtypeStruct((tok_count, share), BF16),
            jax.ShapeDtypeStruct(cache_pages.shape, BF16),
        ),
        in_specs=[vmem] * 7 + [anywhere],
        out_specs=(vmem, anywhere),
        scratch_shapes=[
            pltpu.VMEM((3, RING, RING, CORES * rows, half), BF16),
            pltpu.VMEM((peers, tok_count, width), BF16),
            pltpu.VMEM((CORES, tok_count, width), BF16),
            pltpu.VMEM((CORES, tok_count, 128), F32),
            pltpu.VMEM((CORES, tok_count, width), BF16),
            pltpu.VMEM((CORES, tok_count, width), F32),
            pltpu.VMEM((CORES * tok_count, half), BF16),
            pltpu.VMEM((tp_count, CORES, tok_count, share), BF16),
            pltpu.VMEM((peers, tok_count, share), BF16),
            dma((7,)),
            dma((5, 2)),
            dma((peers, 2)),
            dma((spread, 2)),
            dma((STREAMS, LAST, 2)),
            dma((4, STREAMS, LAST, 2)),
            dma((peers, 2)),
        ],
        compiler_params=pltpu.CompilerParams(
            collective_id=0, has_side_effects=True, vmem_limit_bytes=48 * 1024 * 1024
        ),
    )(part, tokens, factor, norm_gain[None, :], flat(w_gate), flat(w_up), flat(w_down), ranked)


def solution(mesh):
    in_specs = (
        P("req", None),
        P("req", "tp"),
        P("tp", None),
        P(),
        P(None, "req", "tp"),
        P(None, "req", "tp"),
        P(None, "req", "tp"),
        P("req", None),
        P("req", None),
        P("req", None, "tp", None),
        P("req"),
    )
    out_specs = (P("req", "tp"), P("req", None, "tp", None))
    return jax.shard_map(
        on_device, mesh=mesh, in_specs=in_specs, out_specs=out_specs, check_vma=False
    )
```

time: 328 us -> 150 us (0.46)
  waiting for transfers between devices: 226 us -> 0 us
  Pallas kernels: 0 us -> 141 us
  starting transfers between devices: 53.2 us -> 0 us
  matrix products: 17.3 us -> 1.27 us
  between operations: 14.2 us -> 0.79 us
  local copies, waits for them, and re-layouts: 12.7 us -> 5.62 us
    all_gather x3 -> x0, waiting for transfers between devices: 206 us -> none  [gathered_weight(): return lax.all_gather(flat, 'req', axis=0, tiled=True)]
    pallas_call x0 -> x1, Pallas kernels: none -> 141 us  [on_device(): pl.pallas_call(functools.partial(expert_kernel, req_count, tp_count), out...]
    ppermute x13 -> x0, starting transfers between devices: 53 us -> none  [passed_along(): return lax.ppermute(value, axis, pairs)]
    dot_general x3 -> x1, matrix products: 17.3 us -> 1.27 us  [on_device(): jnp.dot(attn_heads, out_proj, preferred_element_type=F32).astype(BF16)]
    reduce_scatter x1 -> x0, waiting for transfers between devices: 15.5 us -> none  [on_device(): lax.psum_scatter(combined.astype(jnp.bfloat16), 'tp', scatter_dimension=1...]
  transfers between devices with their start and end apart: 17 -> 0, of which waited for: 6 -> 0; matrix products, arithmetic and copies ran while one was open for 10% -> 0% of each run, Pallas kernels for 0% -> 0%
where the time goes in v2:
time: 150 us; the launch traced here: 149 us
  Pallas kernels  141 us (94%)
  local copies, waits for them, and re-layouts  5.62 us (4%)
    pallas_call x1, Pallas kernels, on_device(): pl.pallas_call(functools.partial(expert_kernel, req_count, tp_count), out...  141 us
    unnamed x22, local copies, waits for them, and re-layouts  4.01 us

profile of v2, /device:TPU:1, one launch (start us, length us, event | category | flops | bytes accessed | tf_op | source)
XLA Modules:
  0.0 149.4 jit_solution(7003378592214859179)
XLA Ops:
  0.6 0.0 copy-start
  0.6 0.0 copy-start.9
  0.7 0.7 copy-done.9
  1.4 0.1 select_reduce_fusion
  1.5 0.0 copy-start.7
  1.5 0.6 copy-done.7
  2.2 0.7 copy-done.8
  2.9 0.3 select_add_fusion.factor_ref
  3.2 0.5 copy-done.6
  3.7 1.3 convolution_convert_fusion.part_ref
  5.0 0.0 copy-done
  5.0 0.0 copy-start.1
  5.0 0.0 copy-start.2
  5.0 0.0 copy-start.3
  5.1 0.0 copy-start.4
  5.1 0.0 copy-start.5
  5.1 1.6 %gather_fusion = bf16[8,128,2,128]{3,2,1,0:T(2,128)(2,1)S(1)} fusion(bf16[8,128,2,128]{3,2,1,0:T(2,128)(2,1)S(1)} %copy-done, s32[1024]{0:T(1024)S(1)} %pad_clamp_fusion), kind=kCustom, calls=%fused_computation | custom fusion | bytes 1048608 | tf_op jit(solution)/shard_map/gather | solution.py:363
  6.7 0.0 copy-done.1
  6.7 0.0 copy-done.2
  6.7 0.0 copy-done.3
  6.7 0.0 copy-done.4
  6.7 141.2 %shard_map.122 = (bf16[128,256]{1,0:T(8,128)(2,1)S(1)}, bf16[8,128,2,128]{3,2,1,0:T(2,128)(2,1)S(1)}) custom-call(bf16[128,1024]{1,0:T(8,128)(2,1)S(1)} %convolution_convert_fusion.part_ref, bf16[128,1024]{1,0:T(8,128)(2,1)S(1)} %copy-done.1, f32[2,128,128]{2,1,0:T(8,128)S(1)} %select_add_fusion.factor_ref, f32[1,1024]{1,0:T(1,128)S(1)} %bitcast.51, ...), custom_call_target="tpu_custom_call" | custom-call | tf_op jit(solution)/shard_map/pallas_call | solution.py:370
  148.0 0.6 copy.15
  148.6 0.8 copy.16
  (10 shorter events, 0.1 us)
Async XLA Ops:
  0.6 4.4 %copy-start = (bf16[8,128,2,128]{3,2,1,0:T(2,128)(2,1)S(1)}, bf16[8,128,2,128]{3,2,1,0:T(2,128)(2,1)}, u32[]{:S(2)}) copy-start(bf16[8,128,2,128]{3,2,1,0:T(2,128)(2,1)} %param.20) | copy-start | bytes 1572868
  0.6 0.7 copy-start.9
  1.5 0.7 copy-start.7
  2.2 0.7 copy-start.8
  2.9 0.8 copy-start.6
  5.0 1.7 %copy-start.1 = (bf16[128,1024]{1,0:T(8,128)(2,1)S(1)}, bf16[128,1024]{1,0:T(8,128)(2,1)}, u32[]{:S(2)}) copy-start(bf16[128,1024]{1,0:T(8,128)(2,1)} %tokens_ref.1) | copy-start | bytes 786436
  5.0 1.7 %copy-start.2 = (bf16[32,8,128]{2,1,0:T(8,128)(2,1)S(1)}, bf16[32,8,128]{2,1,0:T(8,128)(2,1)}, u32[]{:S(2)}) copy-start(bf16[32,8,128]{2,1,0:T(8,128)(2,1)} %param.15) | copy-start | bytes 196612
  5.0 1.7 %copy-start.3 = (bf16[32,8,128]{2,1,0:T(8,128)(2,1)S(1)}, bf16[32,8,128]{2,1,0:T(8,128)(2,1)}, u32[]{:S(2)}) copy-start(bf16[32,8,128]{2,1,0:T(8,128)(2,1)} %param.16) | copy-start | bytes 196612
  5.1 1.7 %copy-start.4 = (bf16[32,8,128]{2,1,0:T(8,128)(2,1)S(1)}, bf16[32,8,128]{2,1,0:T(8,128)(2,1)}, u32[]{:S(2)}) copy-start(bf16[32,8,128]{2,1,0:T(8,128)(2,1)} %param.17) | copy-start | bytes 196612
  5.1 1.7 %copy-start.5 = (f32[1024]{0:T(1024)S(1)}, f32[1024]{0:T(1024)}, u32[]{:S(2)}) copy-start(f32[1024]{0:T(1024)} %param.14) | copy-start | bytes 12292

commit v3 on v2

--- a/solution.py
+++ b/solution.py
@@ -12,6 +12,8 @@
 CORES = 2
 STREAMS = 4
 LAST = RING - 1
+HOPS = ((4, 3), (3, 4))
+TILES = ((2, 5, 5, 4), (3, 4, 4, 5), (4, 4, 4, 4))
 F32 = jnp.float32
 BF16 = jnp.bfloat16
 
@@ -57,7 +59,6 @@
     chip = me - core
     tok_count, width = tokens_ref.shape
     half = full.shape[4]
-    cut = half // STREAMS
     pages = pages_ref.shape[0]
     share = width // tp_count
 
@@ -122,10 +123,6 @@
         device = peer(lax.rem(mine + step, peers))
         return remote(part_ref, parts.at[mine], part_sem.at[step], device)
 
-    for step in range(1, peers):
-        part_copy(step).start()
-    for step in range(pages - 1, 0, -1):
-        page_copy(step).start()
     for index in range(3):
         swaps[index].wait_recv()
         locals_[index].wait()
@@ -136,45 +133,67 @@
     def forth(place, step):
         return lax.rem(place + step, RING)
 
-    def first_copy(stream, step):
-        columns = pl.ds(stream * cut, cut)
-        y_place, z_place = (
-            (back(y, step), z),
-            (forth(y, step), z),
-            (y, back(z, step)),
-            (y, forth(z, step)),
-        )[stream]
-        device = (ahead_y, behind_y, ahead_z, behind_z)[stream]
-        block = full.at[:, y_place, z_place, :, columns]
-        return remote(block, block, first_sem.at[stream, step], device)
+    def span_of(weight, first, last):
+        start = sum(TILES[weight][:first]) * 128
+        return pl.ds(start, sum(TILES[weight][first:last]) * 128)
+
+    along = ((ahead_y, behind_y), (ahead_z, behind_z))
+
+    def place_of(axis, sign, step):
+        return (back, forth)[sign]((y, z)[axis], step)
+
+    def first_copy(axis, sign, part, step):
+        weights = (pl.ds(0, 2), pl.ds(2, 1))[part]
+        columns = span_of(2 * part, 2 * axis, 2 * axis + 2)
+        place = place_of(axis, sign, step)
+        block = full.at[weights, place, z, :, columns]
+        if axis == 1:
+            block = full.at[weights, y, place, :, columns]
+        return remote(block, block, first_sem.at[axis * 2 + sign, part, step], along[axis][sign])
+
+    def spread(axis, place):
+        for weight in range(2):
+            for sign in range(2):
+                stream = axis * 2 + sign
+                columns = span_of(weight, stream, stream + 1)
+                block = full.at[weight, place, z, :, columns]
+                if axis == 1:
+                    block = full.at[weight, y, place, :, columns]
+                sems = second_sem.at[weight, stream, 0]
+                remote(block, block, sems, along[1 - axis][sign]).start()
 
     def second_copy(piece, stream, step):
         weight = min(piece, 2)
-        size = cut if piece < 2 else cut // 2
-        columns = pl.ds(stream * cut + max(piece - 2, 0) * size, size)
-        device = (ahead_z, behind_z, ahead_y, behind_y)[stream]
-        if stream == 0:
-            block = full.at[weight, :, back(z, step), :, columns]
-        elif stream == 1:
-            block = full.at[weight, :, forth(z, step), :, columns]
-        elif stream == 2:
-            block = full.at[weight, back(y, step), :, :, columns]
-        else:
-            block = full.at[weight, forth(y, step), :, :, columns]
-        return remote(block, block, second_sem.at[piece, stream, step], device)
-
-    def first_step(step, carry):
-        for stream in range(STREAMS):
-            first_copy(stream, step).start()
-        for stream in range(STREAMS):
-            first_copy(stream, step).wait_recv()
-        return carry
-
-    lax.fori_loop(0, LAST, first_step, 0)
-
-    for piece in (0, 1):
-        for stream in range(STREAMS):
-            second_copy(piece, stream, 0).start()
+        columns = span_of(weight, stream, stream + 1)
+        if piece >= 2:
+            size = columns.size // 2
+            columns = pl.ds(columns.start + (piece - 2) * size, size)
+        axis, sign = 1 - stream // 2, stream % 2
+        place = place_of(axis, sign, step)
+        block = full.at[weight, place, :, :, columns]
+        if axis == 1:
+            block = full.at[weight, :, place, :, columns]
+        return remote(block, block, second_sem.at[piece, stream, step], along[axis][sign])
+
+    for part in range(2):
+        for axis in range(2):
+            for sign in range(2):
+                first_copy(axis, sign, part, 0).start()
+    for axis in range(2):
+        spread(axis, (y, z)[axis])
+    for step in range(1, peers):
+        part_copy(step).start()
+    for step in range(1, max(HOPS[0]) + 1):
+        for axis in range(2):
+            for sign in range(2):
+                if step <= HOPS[axis][sign]:
+                    for part in range(2):
+                        first_copy(axis, sign, part, step - 1).wait_recv()
+                        if step < HOPS[axis][sign]:
+                            first_copy(axis, sign, part, step).start()
+                    spread(axis, place_of(axis, sign, step))
+
+    page_copy(pages - 1).start()
 
     def second_step(pieces, step):
         for piece in pieces:
@@ -183,6 +202,7 @@
                 second_copy(piece, stream, step).start()
 
     second_step((0, 1), 1)
+    page_copy(pages - 2).start()
 
     for step in range(1, peers):
         part_copy(step).wait_recv()
@@ -208,6 +228,7 @@
 
     def gate_up_step(step, carry):
         second_step((0, 1), step)
+        page_copy(pages - 1 - step).start()
         return carry
 
     lax.fori_loop(2, LAST, gate_up_step, 0)
@@ -311,9 +332,14 @@
     for step in range(1, pages):
         page_copy(step).wait()
 
+    for axis in range(2):
+        for sign in range(2):
+            for step in range(HOPS[axis][sign]):
+                for part in range(2):
+                    first_copy(axis, sign, part, step).wait_send()
+
     def drain(step, carry):
         for stream in range(STREAMS):
-            first_copy(stream, step).wait_send()
             for piece in range(4):
                 second_copy(piece, stream, step).wait_send()
         return carry
@@ -389,7 +415,7 @@
             dma((5, 2)),
             dma((peers, 2)),
             dma((spread, 2)),
-            dma((STREAMS, LAST, 2)),
+            dma((STREAMS, 2, max(HOPS[0]), 2)),
             dma((4, STREAMS, LAST, 2)),
             dma((peers, 2)),
         ],

time: 150 us -> 129 us (0.86)
  Pallas kernels: 141 us -> 121 us
    pallas_call x1, Pallas kernels: 141 us -> 121 us  [on_device(): pl.pallas_call(functools.partial(expert_kernel, req_count, tp_count), out...]
where the time goes in v3:
time: 129 us
  Pallas kernels  121 us (94%)
  local copies, waits for them, and re-layouts  5.62 us (4%)
    pallas_call x1, Pallas kernels, on_device(): pl.pallas_call(functools.partial(expert_kernel, req_count, tp_count), out...  121 us
    unnamed x22, local copies, waits for them, and re-layouts  4.01 us

profile of v3, /device:TPU:1, one launch (start us, length us, event | category | flops | bytes accessed | tf_op | source)
XLA Modules:
  0.0 128.7 jit_solution(3497645972655847197)
XLA Ops:
  0.6 0.0 copy-start
  0.6 0.0 copy-start.9
  0.7 0.7 copy-done.9
  1.4 0.1 select_reduce_fusion
  1.5 0.0 copy-start.7
  1.5 0.6 copy-done.7
  2.2 0.7 copy-done.8
  2.9 0.3 select_add_fusion.factor_ref
  3.2 0.5 copy-done.6
  3.7 1.3 convolution_convert_fusion.part_ref
  5.0 0.0 copy-done
  5.0 0.0 copy-start.1
  5.0 0.0 copy-start.2
  5.0 0.0 copy-start.3
  5.1 0.0 copy-start.4
  5.1 0.0 copy-start.5
  5.1 1.6 %gather_fusion = bf16[8,128,2,128]{3,2,1,0:T(2,128)(2,1)S(1)} fusion(bf16[8,128,2,128]{3,2,1,0:T(2,128)(2,1)S(1)} %copy-done, s32[1024]{0:T(1024)S(1)} %pad_clamp_fusion), kind=kCustom, calls=%fused_computation | custom fusion | bytes 1048608 | tf_op jit(solution)/shard_map/gather | solution.py:389
  6.7 0.0 copy-done.1
  6.7 0.0 copy-done.2
  6.7 0.0 copy-done.3
  6.7 0.0 copy-done.4
  6.7 120.5 %shard_map.122 = (bf16[128,256]{1,0:T(8,128)(2,1)S(1)}, bf16[8,128,2,128]{3,2,1,0:T(2,128)(2,1)S(1)}) custom-call(bf16[128,1024]{1,0:T(8,128)(2,1)S(1)} %convolution_convert_fusion.part_ref, bf16[128,1024]{1,0:T(8,128)(2,1)S(1)} %copy-done.1, f32[2,128,128]{2,1,0:T(8,128)S(1)} %select_add_fusion.factor_ref, f32[1,1024]{1,0:T(1,128)S(1)} %bitcast.51, ...), custom_call_target="tpu_custom_call" | custom-call | tf_op jit(solution)/shard_map/pallas_call | solution.py:396
  127.3 0.6 copy.15
  127.9 0.8 copy.16
  (10 shorter events, 0.1 us)
Async XLA Ops:
  0.6 4.4 %copy-start = (bf16[8,128,2,128]{3,2,1,0:T(2,128)(2,1)S(1)}, bf16[8,128,2,128]{3,2,1,0:T(2,128)(2,1)}, u32[]{:S(2)}) copy-start(bf16[8,128,2,128]{3,2,1,0:T(2,128)(2,1)} %param.20) | copy-start | bytes 1572868
  0.6 0.7 copy-start.9
  1.5 0.7 copy-start.7
  2.2 0.7 copy-start.8
  2.9 0.8 copy-start.6
  5.0 1.7 %copy-start.1 = (bf16[128,1024]{1,0:T(8,128)(2,1)S(1)}, bf16[128,1024]{1,0:T(8,128)(2,1)}, u32[]{:S(2)}) copy-start(bf16[128,1024]{1,0:T(8,128)(2,1)} %tokens_ref.1) | copy-start | bytes 786436
  5.0 1.7 %copy-start.2 = (bf16[32,8,128]{2,1,0:T(8,128)(2,1)S(1)}, bf16[32,8,128]{2,1,0:T(8,128)(2,1)}, u32[]{:S(2)}) copy-start(bf16[32,8,128]{2,1,0:T(8,128)(2,1)} %param.15) | copy-start | bytes 196612
  5.0 1.7 %copy-start.3 = (bf16[32,8,128]{2,1,0:T(8,128)(2,1)S(1)}, bf16[32,8,128]{2,1,0:T(8,128)(2,1)}, u32[]{:S(2)}) copy-start(bf16[32,8,128]{2,1,0:T(8,128)(2,1)} %param.16) | copy-start | bytes 196612
  5.1 1.7 %copy-start.4 = (bf16[32,8,128]{2,1,0:T(8,128)(2,1)S(1)}, bf16[32,8,128]{2,1,0:T(8,128)(2,1)}, u32[]{:S(2)}) copy-start(bf16[32,8,128]{2,1,0:T(8,128)(2,1)} %param.17) | copy-start | bytes 196612
  5.1 1.7 %copy-start.5 = (f32[1024]{0:T(1024)S(1)}, f32[1024]{0:T(1024)}, u32[]{:S(2)}) copy-start(f32[1024]{0:T(1024)} %param.14) | copy-start | bytes 12292

commit v4 on v3

--- a/solution.py
+++ b/solution.py
@@ -23,7 +23,8 @@
     tp_count,
     part_ref,
     tokens_ref,
-    factor_ref,
+    routes_ref,
+    weights_ref,
     gain_ref,
     gate_ref,
     up_ref,
@@ -34,6 +35,8 @@
     full,
     parts,
     both,
+    named,
+    shares,
     factors,
     normed,
     residual,
@@ -107,11 +110,13 @@
         swaps.append(remote(weight.at[:, given], place, swap_sem.at[index], partner))
         locals_.append(pltpu.make_async_copy(weight.at[:, kept], place, local_sem.at[index]))
     swaps.append(remote(tokens_ref, both.at[core], swap_sem.at[3], partner))
-    swaps.append(remote(factor_ref.at[other], factors.at[core], swap_sem.at[4], partner))
+    swaps.append(remote(routes_ref, named.at[core], swap_sem.at[4], partner))
+    swaps.append(remote(weights_ref, shares.at[core], swap_sem.at[5], partner))
     locals_.append(pltpu.make_async_copy(tokens_ref, both.at[core], local_sem.at[3]))
-    locals_.append(pltpu.make_async_copy(factor_ref.at[core], factors.at[core], local_sem.at[4]))
-    locals_.append(pltpu.make_async_copy(part_ref, parts.at[mine], local_sem.at[5]))
-    locals_.append(pltpu.make_async_copy(pages_ref.at[0], cache_ref.at[0], local_sem.at[6]))
+    locals_.append(pltpu.make_async_copy(routes_ref, named.at[core], local_sem.at[4]))
+    locals_.append(pltpu.make_async_copy(weights_ref, shares.at[core], local_sem.at[5]))
+    locals_.append(pltpu.make_async_copy(part_ref, parts.at[mine], local_sem.at[6]))
+    locals_.append(pltpu.make_async_copy(pages_ref.at[0], cache_ref.at[0], local_sem.at[7]))
     for copy in swaps + locals_:
         copy.start()
 
@@ -166,8 +171,11 @@
         weight = min(piece, 2)
         columns = span_of(weight, stream, stream + 1)
         if piece >= 2:
-            size = columns.size // 2
-            columns = pl.ds(columns.start + (piece - 2) * size, size)
+            size = columns.size // 256 * 128
+            if piece == 2:
+                columns = pl.ds(columns.start, size)
+            else:
+                columns = pl.ds(columns.start + size, columns.size - size)
         axis, sign = 1 - stream // 2, stream % 2
         place = place_of(axis, sign, step)
         block = full.at[weight, place, :, :, columns]
@@ -183,14 +191,16 @@
         spread(axis, (y, z)[axis])
     for step in range(1, peers):
         part_copy(step).start()
+    turns = [(axis, sign) for axis in range(2) for sign in range(2)]
     for step in range(1, max(HOPS[0]) + 1):
-        for axis in range(2):
-            for sign in range(2):
-                if step <= HOPS[axis][sign]:
-                    for part in range(2):
-                        first_copy(axis, sign, part, step - 1).wait_recv()
-                        if step < HOPS[axis][sign]:
-                            first_copy(axis, sign, part, step).start()
+        here = [turn for turn in turns if step <= HOPS[turn[0]][turn[1]]]
+        for part in range(2):
+            for axis, sign in here:
+                first_copy(axis, sign, part, step - 1).wait_recv()
+                if step < HOPS[axis][sign]:
+                    first_copy(axis, sign, part, step).start()
+            if part == 0:
+                for axis, sign in here:
                     spread(axis, place_of(axis, sign, step))
 
     page_copy(pages - 1).start()
@@ -206,11 +216,21 @@
 
     for step in range(1, peers):
         part_copy(step).wait_recv()
-    for index in (3, 4):
+    for index in (3, 4, 5):
         swaps[index].wait_recv()
-    for index in (3, 4, 5):
+    for index in (3, 4, 5, 6):
         locals_[index].wait()
     lines = 32
+
+    own = half // 128
+    ids = lax.broadcasted_iota(jnp.int32, (128, tok_count), 0)
+    ids = jnp.where(ids < own, ids + core * own, -1)
+    for which in range(CORES):
+        table = jnp.zeros((128, tok_count), F32)
+        for route in range(named.shape[1]):
+            hit = named[which, route : route + 1, :] == ids
+            table = table + jnp.where(hit, shares[which, route : route + 1, :], 0.0)
+        factors[which] = table.T
 
     def norm_step(step, carry):
         which = step // (tok_count // lines)
@@ -328,7 +348,7 @@
         part_copy(step).wait_send()
     for copy in swaps:
         copy.wait_send()
-    locals_[6].wait()
+    locals_[7].wait()
     for step in range(1, pages):
         page_copy(step).wait()
 
@@ -372,15 +392,6 @@
 
     part = jnp.dot(attn_heads, out_proj, preferred_element_type=F32).astype(BF16)
 
-    lanes = jnp.arange(128, dtype=jnp.int32)
-    own = experts // CORES
-    ids = jnp.stack([jnp.where(lanes < own, lanes + h * own, -1) for h in range(CORES)])
-    factor = jnp.zeros((CORES, tok_count, 128), F32)
-    for route in range(top_count):
-        factor = factor + jnp.where(
-            routes[None, :, route, None] == ids[:, None, :], gate_weights[None, :, route, None], 0.0
-        )
-
     spread = cache_pages.shape[0]
     places = jnp.arange(spread, dtype=jnp.int32)
     page_order = jnp.sum(
@@ -399,20 +410,22 @@
             jax.ShapeDtypeStruct((tok_count, share), BF16),
             jax.ShapeDtypeStruct(cache_pages.shape, BF16),
         ),
-        in_specs=[vmem] * 7 + [anywhere],
+        in_specs=[vmem] * 8 + [anywhere],
         out_specs=(vmem, anywhere),
         scratch_shapes=[
             pltpu.VMEM((3, RING, RING, CORES * rows, half), BF16),
             pltpu.VMEM((peers, tok_count, width), BF16),
             pltpu.VMEM((CORES, tok_count, width), BF16),
+            pltpu.VMEM((CORES, top_count, tok_count), jnp.int32),
+            pltpu.VMEM((CORES, top_count, tok_count), F32),
             pltpu.VMEM((CORES, tok_count, 128), F32),
             pltpu.VMEM((CORES, tok_count, width), BF16),
             pltpu.VMEM((CORES, tok_count, width), F32),
             pltpu.VMEM((CORES * tok_count, half), BF16),
             pltpu.VMEM((tp_count, CORES, tok_count, share), BF16),
             pltpu.VMEM((peers, tok_count, share), BF16),
-            dma((7,)),
-            dma((5, 2)),
+            dma((8,)),
+            dma((6, 2)),
             dma((peers, 2)),
             dma((spread, 2)),
             dma((STREAMS, 2, max(HOPS[0]), 2)),
@@ -422,7 +435,7 @@
         compiler_params=pltpu.CompilerParams(
             collective_id=0, has_side_effects=True, vmem_limit_bytes=48 * 1024 * 1024
         ),
-    )(part, tokens, factor, norm_gain[None, :], flat(w_gate), flat(w_up), flat(w_down), ranked)
+    )(part, tokens, routes.T, gate_weights.T, norm_gain[None, :], flat(w_gate), flat(w_up), flat(w_down), ranked)
 
 
 def solution(mesh):

time: 129 us -> 125 us (0.969)
  Pallas kernels: 121 us -> 119 us
  local copies, waits for them, and re-layouts: 5.62 us -> 3.79 us
    pallas_call x1, Pallas kernels: 121 us -> 119 us  [on_device(): pl.pallas_call(functools.partial(expert_kernel, req_count, tp_count), out...]
    unnamed x22 -> x20, local copies, waits for them, and re-layouts: 4.01 us -> 2.18 us
where the time goes in v4:
time: 125 us
  Pallas kernels  119 us (95%)
  local copies, waits for them, and re-layouts  3.79 us (3%)
  matrix products  1.32 us (1%)
    pallas_call x1, Pallas kernels, on_device(): pl.pallas_call(functools.partial(expert_kernel, req_count, tp_count), out...  119 us

profile of v4, /device:TPU:1, one launch (start us, length us, event | category | flops | bytes accessed | tf_op | source)
XLA Modules:
  0.0 124.6 jit_solution(11141893968795048967)
XLA Ops:
  0.6 0.0 copy-start
  0.6 0.0 copy-start.8
  0.7 0.7 copy-done.8
  1.4 0.1 select_reduce_fusion
  1.5 1.3 %convolution_convert_fusion.part_ref = bf16[128,1024]{1,0:T(8,128)(2,1)S(1)} fusion(bf16[128,256]{1,0:T(8,128)(2,1)} %param.12, bf16[256,1024]{1,0:T(8,128)(2,1)} %param.13), kind=kOutput, calls=%fused_computation.1 | convolution fusion | flops 67239936 | bytes 851968 | tf_op jit(solution)/shard_map/dot_general | solution.py:393
  2.8 0.0 copy-done
  2.8 0.0 copy-start.1
  2.8 0.0 copy-start.2
  2.9 0.0 copy-start.3
  2.9 0.0 copy-start.4
  2.9 0.0 copy-start.5
  2.9 0.0 copy-start.6
  2.9 0.0 copy-start.7
  2.9 1.6 %gather_fusion = bf16[8,128,2,128]{3,2,1,0:T(2,128)(2,1)S(1)} fusion(bf16[8,128,2,128]{3,2,1,0:T(2,128)(2,1)S(1)} %copy-done, s32[1024]{0:T(1024)S(1)} %pad_clamp_fusion), kind=kCustom, calls=%fused_computation | custom fusion | bytes 1048608 | tf_op jit(solution)/shard_map/gather | solution.py:400
  4.5 0.0 copy-done.1
  4.5 0.0 copy-done.2
  4.6 0.0 copy-done.3
  4.6 0.0 copy-done.4
  4.6 0.0 copy-done.5
  4.6 0.0 copy-done.6
  4.6 0.0 copy-done.7
  4.6 118.6 %shard_map.122 = (bf16[128,256]{1,0:T(8,128)(2,1)S(1)}, bf16[8,128,2,128]{3,2,1,0:T(2,128)(2,1)S(1)}) custom-call(bf16[128,1024]{1,0:T(8,128)(2,1)S(1)} %convolution_convert_fusion.part_ref, bf16[128,1024]{1,0:T(8,128)(2,1)S(1)} %copy-done.1, s32[8,128]{1,0:T(8,128)S(1)} %bitcast.21, f32[8,128]{1,0:T(8,128)S(1)} %bitcast.22, f32[1,1024]{1,0:T(1,128)S(1)} %bitcast.23, ...), custom_call_target="tpu_custom_call" | custom-call | tf_op jit(solution)/shard_map/pallas_call | solution.py:407
  123.2 0.6 copy.15
  123.8 0.8 copy.16
  (3 shorter events, 0.0 us)
Async XLA Ops:
  0.6 2.2 %copy-start = (bf16[8,128,2,128]{3,2,1,0:T(2,128)(2,1)S(1)}, bf16[8,128,2,128]{3,2,1,0:T(2,128)(2,1)}, u32[]{:S(2)}) copy-start(bf16[8,128,2,128]{3,2,1,0:T(2,128)(2,1)} %param.20) | copy-start | bytes 1572868
  0.6 0.7 copy-start.8
  2.8 1.7 %copy-start.1 = (bf16[128,1024]{1,0:T(8,128)(2,1)S(1)}, bf16[128,1024]{1,0:T(8,128)(2,1)}, u32[]{:S(2)}) copy-start(bf16[128,1024]{1,0:T(8,128)(2,1)} %tokens_ref.1) | copy-start | bytes 786436
  2.8 1.7 %copy-start.2 = (bf16[32,8,128]{2,1,0:T(8,128)(2,1)S(1)}, bf16[32,8,128]{2,1,0:T(8,128)(2,1)}, u32[]{:S(2)}) copy-start(bf16[32,8,128]{2,1,0:T(8,128)(2,1)} %param.15) | copy-start | bytes 196612
  2.9 1.7 %copy-start.3 = (bf16[32,8,128]{2,1,0:T(8,128)(2,1)S(1)}, bf16[32,8,128]{2,1,0:T(8,128)(2,1)}, u32[]{:S(2)}) copy-start(bf16[32,8,128]{2,1,0:T(8,128)(2,1)} %param.16) | copy-start | bytes 196612
  2.9 1.7 %copy-start.4 = (bf16[32,8,128]{2,1,0:T(8,128)(2,1)S(1)}, bf16[32,8,128]{2,1,0:T(8,128)(2,1)}, u32[]{:S(2)}) copy-start(bf16[32,8,128]{2,1,0:T(8,128)(2,1)} %param.17) | copy-start | bytes 196612
  2.9 1.7 %copy-start.5 = (s32[128,8]{0,1:T(8,128)S(1)}, s32[128,8]{0,1:T(8,128)}, u32[]{:S(2)}) copy-start(s32[128,8]{0,1:T(8,128)} %param.18) | copy-start | bytes 12292
  2.9 1.7 %copy-start.6 = (f32[128,8]{0,1:T(8,128)S(1)}, f32[128,8]{0,1:T(8,128)}, u32[]{:S(2)}) copy-start(f32[128,8]{0,1:T(8,128)} %param.19) | copy-start | bytes 12292
  2.9 1.7 %copy-start.7 = (f32[1024]{0:T(1024)S(1)}, f32[1024]{0:T(1024)}, u32[]{:S(2)}) copy-start(f32[1024]{0:T(1024)} %param.14) | copy-start | bytes 12292

commit v5 on v4

--- a/solution.py
+++ b/solution.py
@@ -206,10 +206,11 @@
     page_copy(pages - 1).start()
 
     def second_step(pieces, step):
-        for piece in pieces:
-            for stream in range(STREAMS):
-                second_copy(piece, stream, step - 1).wait_recv()
-                second_copy(piece, stream, step).start()
+        for streams in ((1, 2, 3), (0,)):
+            for piece in pieces:
+                for stream in streams:
+                    second_copy(piece, stream, step - 1).wait_recv()
+                    second_copy(piece, stream, step).start()
 
     second_step((0, 1), 1)
     page_copy(pages - 2).start()

time: 125 us -> 126 us (level)
    pallas_call x1, Pallas kernels: 119 us -> 120 us  [on_device(): pl.pallas_call(functools.partial(expert_kernel, req_count, tp_count), out...]
where the time goes in v5:
time: 126 us
  Pallas kernels  120 us (95%)
  local copies, waits for them, and re-layouts  3.79 us (3%)
  matrix products  1.32 us (1%)
    pallas_call x1, Pallas kernels, on_device(): pl.pallas_call(functools.partial(expert_kernel, req_count, tp_count), out...  120 us

profile of v5, /device:TPU:1, one launch (start us, length us, event | category | flops | bytes accessed | tf_op | source)
XLA Modules:
  0.0 126.1 jit_solution(4250148488880380775)
XLA Ops:
  0.6 0.0 copy-start
  0.6 0.0 copy-start.8
  0.7 0.7 copy-done.8
  1.4 0.1 select_reduce_fusion
  1.5 1.3 %convolution_convert_fusion.part_ref = bf16[128,1024]{1,0:T(8,128)(2,1)S(1)} fusion(bf16[128,256]{1,0:T(8,128)(2,1)} %param.12, bf16[256,1024]{1,0:T(8,128)(2,1)} %param.13), kind=kOutput, calls=%fused_computation.1 | convolution fusion | flops 67239936 | bytes 851968 | tf_op jit(solution)/shard_map/dot_general | solution.py:394
  2.8 0.0 copy-done
  2.8 0.0 copy-start.1
  2.8 0.0 copy-start.2
  2.9 0.0 copy-start.3
  2.9 0.0 copy-start.4
  2.9 0.0 copy-start.5
  2.9 0.0 copy-start.6
  2.9 0.0 copy-start.7
  2.9 1.6 %gather_fusion = bf16[8,128,2,128]{3,2,1,0:T(2,128)(2,1)S(1)} fusion(bf16[8,128,2,128]{3,2,1,0:T(2,128)(2,1)S(1)} %copy-done, s32[1024]{0:T(1024)S(1)} %pad_clamp_fusion), kind=kCustom, calls=%fused_computation | custom fusion | bytes 1048608 | tf_op jit(solution)/shard_map/gather | solution.py:401
  4.5 0.0 copy-done.1
  4.5 0.0 copy-done.2
  4.6 0.0 copy-done.3
  4.6 0.0 copy-done.4
  4.6 0.0 copy-done.5
  4.6 0.0 copy-done.6
  4.6 0.0 copy-done.7
  4.6 120.1 %shard_map.122 = (bf16[128,256]{1,0:T(8,128)(2,1)S(1)}, bf16[8,128,2,128]{3,2,1,0:T(2,128)(2,1)S(1)}) custom-call(bf16[128,1024]{1,0:T(8,128)(2,1)S(1)} %convolution_convert_fusion.part_ref, bf16[128,1024]{1,0:T(8,128)(2,1)S(1)} %copy-done.1, s32[8,128]{1,0:T(8,128)S(1)} %bitcast.21, f32[8,128]{1,0:T(8,128)S(1)} %bitcast.22, f32[1,1024]{1,0:T(1,128)S(1)} %bitcast.23, ...), custom_call_target="tpu_custom_call" | custom-call | tf_op jit(solution)/shard_map/pallas_call | solution.py:408
  124.7 0.6 copy.15
  125.3 0.8 copy.16
  (3 shorter events, 0.0 us)
Async XLA Ops:
  0.6 2.2 %copy-start = (bf16[8,128,2,128]{3,2,1,0:T(2,128)(2,1)S(1)}, bf16[8,128,2,128]{3,2,1,0:T(2,128)(2,1)}, u32[]{:S(2)}) copy-start(bf16[8,128,2,128]{3,2,1,0:T(2,128)(2,1)} %param.20) | copy-start | bytes 1572868
  0.6 0.7 copy-start.8
  2.8 1.7 %copy-start.1 = (bf16[128,1024]{1,0:T(8,128)(2,1)S(1)}, bf16[128,1024]{1,0:T(8,128)(2,1)}, u32[]{:S(2)}) copy-start(bf16[128,1024]{1,0:T(8,128)(2,1)} %tokens_ref.1) | copy-start | bytes 786436
  2.8 1.7 %copy-start.2 = (bf16[32,8,128]{2,1,0:T(8,128)(2,1)S(1)}, bf16[32,8,128]{2,1,0:T(8,128)(2,1)}, u32[]{:S(2)}) copy-start(bf16[32,8,128]{2,1,0:T(8,128)(2,1)} %param.15) | copy-start | bytes 196612
  2.9 1.7 %copy-start.3 = (bf16[32,8,128]{2,1,0:T(8,128)(2,1)S(1)}, bf16[32,8,128]{2,1,0:T(8,128)(2,1)}, u32[]{:S(2)}) copy-start(bf16[32,8,128]{2,1,0:T(8,128)(2,1)} %param.16) | copy-start | bytes 196612
  2.9 1.7 %copy-start.4 = (bf16[32,8,128]{2,1,0:T(8,128)(2,1)S(1)}, bf16[32,8,128]{2,1,0:T(8,128)(2,1)}, u32[]{:S(2)}) copy-start(bf16[32,8,128]{2,1,0:T(8,128)(2,1)} %param.17) | copy-start | bytes 196612
  2.9 1.7 %copy-start.5 = (s32[128,8]{0,1:T(8,128)S(1)}, s32[128,8]{0,1:T(8,128)}, u32[]{:S(2)}) copy-start(s32[128,8]{0,1:T(8,128)} %param.18) | copy-start | bytes 12292
  2.9 1.7 %copy-start.6 = (f32[128,8]{0,1:T(8,128)S(1)}, f32[128,8]{0,1:T(8,128)}, u32[]{:S(2)}) copy-start(f32[128,8]{0,1:T(8,128)} %param.19) | copy-start | bytes 12292
  2.9 1.7 %copy-start.7 = (f32[1024]{0:T(1024)S(1)}, f32[1024]{0:T(1024)}, u32[]{:S(2)}) copy-start(f32[1024]{0:T(1024)} %param.14) | copy-start | bytes 12292
